TPU v7x, 768 devices: a whole 4x8x12 slice. The times are simulated.
768 devices in a mesh: cuts: 8 (over x, core), stem: 16 (over y, z_hi), rep: 6 (over z_lo).
Axes of the slice: x: 4, y: 8, z: 12 (z_hi: 2, z_lo: 6; z = z_hi * 6 + z_lo), core: 2. Of those that a mesh axis runs over, the one named last changes fastest.
Arguments:
- stem_slabs: bfloat16 [16, 1728, 1728], P('cuts', 'stem'), may hold values from -6 to 6
- site_first: bfloat16 [16, 1728, 1728], P('cuts', 'rep'), may hold values from -0.15625 to 0.15625
- site_second: bfloat16 [16, 1728, 1728], P('cuts', 'rep'), may hold values from -0.15625 to 0.15625
- environment: bfloat16 [16, 8], P('cuts'), may hold values from -2 to 2
Outputs:
- next_stem: bfloat16 [8, 1728, 1728], P('cuts', 'stem')
All inputs are finite; a program needn't handle non-finite values.
Results may differ from a plain program's by a relative error of at most 0.0057.
Values may be sent and summed in bfloat16 or wider, within the bound.
No kernel may reach another device: no remote copies, remote signals or barrier semaphores. Data moves between devices by JAX's collectives and lax.ppermute only.
A program may use at most 32 MiB of HBM per device.

v0:
```python
import jax
import jax.numpy as jnp
from jax import lax
from jax.experimental import pallas as pl
from jax.experimental.pallas import tpu as pltpu
from jax.sharding import Mesh, PartitionSpec as P


U, V, HI, PAIRS, DUO = 4, 2, 2, 3, 2
LANES = 128
SWAP = [(0, 1), (1, 0)]
REP = ("pair", "duo")
Z = ("hi", *REP)
F32, BF16 = jnp.float32, jnp.bfloat16


def spread(block, axis, n):
    return lax.all_to_all(
        jnp.broadcast_to(block[None], (n, *block.shape)), axis, 0, 0, tiled=True
    )


def pick(array, index):
    return lax.dynamic_index_in_dim(array, index, 0, keepdims=False)


def pieces_of(owner, rows, share, n_rep):
    found = []
    for block in range(U):
        begin, filled = rows * (V * HI * block + owner), 0
        for rep in range(n_rep):
            low, high = max(begin, share * rep), min(begin + rows, share * (rep + 1))
            if low < high:
                window = min(max(begin - share * rep, 0), share - rows)
                found.append((block, filled, rep, low - share * rep - window, high - low))
                filled += high - low
    return found


def folded(value, used):
    rows, lanes = value.shape
    whole, rest = lanes // LANES, lanes % LANES
    fold = LANES // rest
    deep = rows // fold
    left = value[:, whole * LANES :]
    side = [left[n * deep : (n + 1) * deep] for n in range(fold)]
    if fold * rest < LANES:
        side.append(jnp.zeros((deep, LANES - fold * rest), value.dtype))
    packed = [value[:, n * LANES : (n + 1) * LANES] for n in range(whole)]
    packed.append(jnp.concatenate(side, axis=1))
    if used > whole * rows + deep:
        packed.append(jnp.zeros((used - whole * rows - deep, LANES), value.dtype))
    return jnp.concatenate(packed, axis=0)


def unfolded(packed, rows, lanes):
    whole, rest = lanes // LANES, lanes % LANES
    fold = LANES // rest
    left = packed[whole * rows : whole * rows + rows // fold]
    left = jnp.concatenate([left[:, n * rest : (n + 1) * rest] for n in range(fold)], axis=0)
    return jnp.concatenate([packed[n * rows : (n + 1) * rows] for n in range(whole)] + [left], axis=1)


def fold_size(rows, lanes):
    return -(-(lanes // LANES * rows + rows // (LANES // (lanes % LANES))) // 8) * 8


def pack(*refs):
    out_ref = refs[-1]
    for side in range(HI):
        for duo in range(DUO):
            packed = folded(refs[side][duo].astype(F32), out_ref.shape[2])
            out_ref[duo, side] = packed.astype(BF16)


def multiply(where_ref, here_ref, below_ref, above_ref, first_ref, out_ref, window_ref, second_ref):
    n_rep = window_ref.shape[0]
    rows, depth = second_ref.shape[1:]
    share = first_ref.shape[1]
    for place, ref in enumerate((here_ref, below_ref, above_ref)):
        for duo in range(DUO):
            window_ref[DUO * where_ref[1 + place] + duo] = unfolded(
                ref[duo].astype(F32), rows, depth
            ).astype(BF16)
    for owner in range(V * HI):

        @pl.when(where_ref[0] == owner)
        def _():
            for block, row, rep, held, count in pieces_of(owner, rows, share, n_rep):
                second_ref[block, row : row + count] = window_ref[rep, held : held + count]

    for block in range(second_ref.shape[0]):
        for duo in range(DUO):
            got = lax.dot_general(
                second_ref[block], first_ref[duo], (((1,), (1,)), ((), ())),
                preferred_element_type=F32,
            )
            out_ref[block * DUO + duo] = folded(got, out_ref.shape[1]).astype(BF16)


def unpack(packed_ref, out_ref):
    n_rep, rows = packed_ref.shape[0], out_ref.shape[0]
    share = out_ref.shape[1] // n_rep
    columns = [unfolded(packed_ref[rep].astype(F32), rows, share) for rep in range(n_rep)]
    out_ref[...] = jnp.concatenate(columns, axis=1).astype(BF16)


def body(stem_slabs, site_first, site_second, environment):
    slices, rows, width = stem_slabs.shape
    share = site_first.shape[1]
    n_rep = PAIRS * DUO
    u, v, hi, rep, pair, duo = (lax.axis_index(a) for a in ("u", "v", "hi", REP, *REP))
    vmem = pl.BlockSpec(memory_space=pltpu.VMEM)
    params = pltpu.CompilerParams(vmem_limit_bytes=12 << 20)

    first = jnp.einsum(
        "cil,cjl->cij", site_first, stem_slabs, preferred_element_type=F32
    ).astype(BF16)
    even, odd = pick(first, duo), pick(first, 1 - duo)

    depth = V * HI * rows
    windows = []
    for side in range(HI):
        owner = HI * v + side
        block = lax.div(share * rep + (V * HI - 1) * rows - rows * owner, V * HI * rows)
        at = jnp.clip(rows * (owner + V * HI * block) - share * rep, 0, share - rows)
        windows.append(lax.dynamic_slice(site_second, (0, at, depth * u), (slices, rows, depth)))
    windows = pl.pallas_call(
        pack,
        out_shape=jax.ShapeDtypeStruct((DUO, HI, fold_size(rows, depth), LANES), BF16),
        in_specs=[vmem, vmem],
        out_specs=vmem,
        compiler_params=params,
    )(*windows)
    kept = pick(windows, duo)
    taken = lax.ppermute(pick(windows, 1 - duo), "duo", SWAP)
    windows = jnp.stack(
        [jnp.where(duo == 0, kept, taken), jnp.where(duo == 0, taken, kept)], axis=1
    )
    where = [HI * v + hi, pair, (pair + PAIRS - 1) % PAIRS, (pair + 1) % PAIRS]

    near = lax.ppermute(odd, "duo", SWAP)
    own = jnp.concatenate(
        [jnp.where(duo == 0, even, near), jnp.where(duo == 0, near, even)], axis=0
    )
    other = lax.ppermute(own, "hi", SWAP)
    ring = HI * n_rep
    up = jnp.where(pair < PAIRS - 1, hi, 1 - hi)
    down = jnp.where(pair > 0, hi, 1 - hi)
    turn = [(i, (i + DUO) % ring) for i in range(ring)]
    below = lax.ppermute(pick(windows, up), Z, turn)
    above = lax.ppermute(pick(windows, down), Z, [(j, i) for i, j in turn])
    own = jnp.concatenate(
        [jnp.where(hi == 0, own, other), jnp.where(hi == 0, other, own)], axis=1
    )
    other = lax.ppermute(own, "v", SWAP)
    first = jnp.concatenate(
        [jnp.where(v == 0, own, other), jnp.where(v == 0, other, own)], axis=1
    ).reshape(DUO, share, depth)

    deep = fold_size(rows, share)
    part = pl.pallas_call(
        multiply,
        out_shape=jax.ShapeDtypeStruct((U * DUO, deep, LANES), BF16),
        in_specs=[pl.BlockSpec(memory_space=pltpu.SMEM), vmem, vmem, vmem, vmem],
        out_specs=vmem,
        scratch_shapes=[
            pltpu.VMEM((n_rep, rows, depth), BF16),
            pltpu.VMEM((U, rows, depth), BF16),
        ],
        compiler_params=params,
    )(jnp.stack(where).astype(jnp.int32), pick(windows, hi), below, above, first)
    part = lax.all_to_all(part, ("u", "duo"), 0, 0, tiled=True)
    part = part.reshape(U, DUO, deep, LANES).astype(F32).sum(0)
    weights = environment.astype(F32)[:, :, None, None]
    terms = sum(weights[c] * part[c] for c in range(slices)).astype(BF16)
    terms = lax.all_to_all(terms, ("x", "core"), 0, 0, tiled=True)
    closed = jnp.sum(terms.astype(F32), 0).astype(BF16)
    whole = spread(closed, REP, n_rep)
    return pl.pallas_call(
        unpack,
        out_shape=jax.ShapeDtypeStruct((rows, width), BF16),
        in_specs=[vmem],
        out_specs=vmem,
        compiler_params=params,
    )(whole)[None]


def solution(mesh):
    fine = Mesh(
        mesh.devices.reshape(4, 2, U, V, HI, PAIRS, DUO),
        ("x", "core", "u", "v", "hi", *REP),
    )
    cuts, stem = ("x", "core"), ("u", "v", "hi")
    placed = (P(cuts, stem, None), P(cuts, REP, None), P(cuts, REP, None), P(cuts, None))
    return jax.shard_map(
        body, mesh=fine, in_specs=placed, out_specs=P(cuts, stem, None), check_vma=False
    )
```

profile of v0, /device:TPU:1, one launch (start us, length us, event | category | flops | bytes accessed | tf_op | source)
XLA Modules:
  0.0 118.2 jit_solution(2712860829000949369)
XLA Ops:
  0.0 0.0 copy-start
  0.0 1.6 %copy-done = bf16[2,288,1728]{2,1,0:T(8,128)(2,1)S(1)} copy-done((bf16[2,288,1728]{2,1,0:T(8,128)(2,1)S(1)}, bf16[2,288,1728]{2,1,0:T(8,128)(2,1)}, u32[]{:S(2)}) %copy-start) | copy-done | bytes 1990680
  1.6 1.8 %convolution_convert_fusion = bf16[2,288,108]{2,1,0:T(8,128)(2,1)S(1)} fusion(bf16[2,288,1728]{2,1,0:T(8,128)(2,1)S(1)} %copy-done, bf16[2,108,1728]{2,0,1:T(2,128)(2,1)} %param.4), kind=kOutput, calls=%fused_computation | convolution fusion | flops 215053056 | bytes 2861568 | tf_op jit(solution)/shard_map/cil,cjl->cij/dot_general | solution.py:116
  3.4 4.8 %collective-permute-start.3 = (bf16[288,108]{1,0:T(8,128)(2,1)S(1)}, bf16[288,108]{1,0:T(8,128)(2,1)S(1)}, u32[]{:S(2)}, u32[]{:S(2)}) collective-permute-start(bf16[288,108]{1,0:T(8,128)(2,1)S(1)} %dynamic-slice_bitcast_fusion.1), channel_id=1, source_target_pairs={{0,1},{1,0},{2,3},{3,2},{4,5},{5,4},{6,7},{7,6},{8,9},{9,8},{10,11... | collective-permute-start | bytes 186632 | tf_op jit(solution)/shard_map/ppermute | solution.py:142
  8.3 1.3 %constant_dynamic-slice_fusion = (bf16[2,108,432]{2,1,0:T(8,128)(2,1)S(1)}, bf16[2,108,432]{2,1,0:T(8,128)(2,1)S(1)}) fusion(bf16[2,288,1728]{2,1,0:T(8,128)(2,1)} %param.6, s32[]{:T(128)S(6)} %min.8, s32[]{:T(128)S(6)} %select_n.93, s32[]{:T(128)S(6)} %min.7), kind=kLoop, calls=%fused_computation.33 | loop fusion | bytes 746508 | tf_op jit(solution)/shard_map/dynamic_slice | solution.py:127
  9.7 0.1 shard_map.46
  9.8 0.2 collective-permute-done.3
  10.0 14.6 %collective-permute-start.4 = (bf16[576,108]{1,0:T(8,128)(2,1)S(1)}, bf16[576,108]{1,0:T(8,128)(2,1)S(1)}, u32[]{:S(2)}, u32[]{:S(2)}) collective-permute-start(bf16[576,108]{1,0:T(8,128)(2,1)S(1)} %pad_maximum_fusion.2), channel_id=1, source_target_pairs={{0,6},{6,0},{1,7},{7,1},{2,8},{8,2},{3,9},{9,3},{4,10},{10,4},{5,1... | collective-permute-start | bytes 373256 | tf_op jit(solution)/shard_map/ppermute | solution.py:146
  24.7 2.8 %collective-permute-start = (bf16[2,384,128]{2,1,0:T(8,128)(2,1)S(1)}, bf16[2,384,128]{2,1,0:T(8,128)(2,1)S(1)}, u32[]{:S(2)}, u32[]{:S(2)}) collective-permute-start(bf16[2,384,128]{2,1,0:T(8,128)(2,1)S(1)} %dynamic-slice_bitcast_fusion), channel_id=1, source_target_pairs={{0,1},{1,0},{2,3},{3,2},{4,5},{5,4},{6,7},{7,6},{8,9},{9,8},{10,11... | collective-permute-start | bytes 589832 | tf_op jit(solution)/shard_map/ppermute | solution.py:136
  27.5 0.1 pad_add_fusion.where_ref
  27.6 0.0 collective-permute-done.4
  27.6 0.1 broadcast_select_fusion.3
  27.6 0.1 pad_maximum_fusion.1
  27.8 3.2 %collective-permute-start.5 = (bf16[576,216]{1,0:T(8,128)(2,1)S(1)}, bf16[576,216]{1,0:T(8,128)(2,1)S(1)}, u32[]{:S(2)}, u32[]{:S(2)}) collective-permute-start(bf16[576,216]{1,0:T(8,128)(2,1)S(1)} %pad_maximum_fusion.1), channel_id=1, source_target_pairs={{0,12},{12,0},{1,13},{13,1},{2,14},{14,2},{3,15},{15,3},{4,16},{16... | collective-permute-start | bytes 746504 | tf_op jit(solution)/shard_map/ppermute | solution.py:156
  31.0 8.0 %collective-permute-done = bf16[2,384,128]{2,1,0:T(8,128)(2,1)S(1)} collective-permute-done((bf16[2,384,128]{2,1,0:T(8,128)(2,1)S(1)}, bf16[2,384,128]{2,1,0:T(8,128)(2,1)S(1)}, u32[]{:S(2)}, u32[]{:S(2)}) %collective-permute-start) | collective-permute-done | bytes 196640 | tf_op jit(solution)/shard_map/ppermute | solution.py:136
  39.1 0.1 fusion.2
  39.2 2.4 %collective-permute-start.1 = (bf16[2,384,128]{2,1,0:T(8,128)(2,1)S(1)}, bf16[2,384,128]{2,1,0:T(8,128)(2,1)S(1)}, u32[]{:S(2)}, u32[]{:S(2)}) collective-permute-start(bf16[2,384,128]{2,1,0:T(8,128)(2,1)S(1)} %get-tuple-element.13), channel_id=1, source_target_pairs={{0,2},{1,3},{2,4},{3,5},{4,6},{5,7},{6,8},{7,9},{8,10},{9,11},{10,... | collective-permute-start | bytes 589832 | tf_op jit(solution)/shard_map/ppermute | solution.py:151
  41.5 7.1 %collective-permute-start.2 = (bf16[2,384,128]{2,1,0:T(8,128)(2,1)S(1)}, bf16[2,384,128]{2,1,0:T(8,128)(2,1)S(1)}, u32[]{:S(2)}, u32[]{:S(2)}) collective-permute-start(bf16[2,384,128]{2,1,0:T(8,128)(2,1)S(1)} %get-tuple-element.11), channel_id=1, source_target_pairs={{2,0},{3,1},{4,2},{5,3},{6,4},{7,5},{8,6},{9,7},{10,8},{11,9},{0,1... | collective-permute-start | bytes 589832 | tf_op jit(solution)/shard_map/ppermute | solution.py:152
  48.7 0.0 collective-permute-done.5
  48.7 0.3 broadcast_select_fusion.1
  49.0 0.0 copy-start.1
  49.0 0.2 pad_maximum_fusion
  49.2 2.1 %collective-permute-done.1.below_ref = bf16[2,384,128]{2,1,0:T(8,128)(2,1)S(1)} collective-permute-done((bf16[2,384,128]{2,1,0:T(8,128)(2,1)S(1)}, bf16[2,384,128]{2,1,0:T(8,128)(2,1)S(1)}, u32[]{:S(2)}, u32[]{:S(2)}) %collective-permute-start.1) | collective-permute-done | bytes 196640 | tf_op jit(solution)/shard_map/ppermute | solution.py:151
  51.3 4.6 %collective-permute-done.2.above_ref = bf16[2,384,128]{2,1,0:T(8,128)(2,1)S(1)} collective-permute-done((bf16[2,384,128]{2,1,0:T(8,128)(2,1)S(1)}, bf16[2,384,128]{2,1,0:T(8,128)(2,1)S(1)}, u32[]{:S(2)}, u32[]{:S(2)}) %collective-permute-start.2) | collective-permute-done | bytes 196640 | tf_op jit(solution)/shard_map/ppermute | solution.py:152
  55.9 2.6 %shard_map.47 = bf16[8,248,128]{2,1,0:T(8,128)(2,1)} custom-call(s32[4]{0:T(128)S(1)} %pad_add_fusion.where_ref, bf16[2,384,128]{2,1,0:T(8,128)(2,1)S(1)} %get-tuple-element.12.here_ref, bf16[2,384,128]{2,1,0:T(8,128)(2,1)S(1)} %collective-permute-done.1.below_ref, bf16[2,384,128]{2,1,0:T(8,128)(2,1)S(1)} %collective-permute-done.2.above_ref, ...), custom_call_target="tpu_custom_call" | custom-call | tf_op jit(solution)/shard_map/pallas_call | solution.py:162
  58.5 7.8 %all-to-all-start = ((bf16[8,248,128]{2,1,0:T(8,128)(2,1)}), bf16[8,248,128]{2,1,0:T(8,128)(2,1)S(1)}, u32[]{:S(2)}, u32[]{:S(2)}) async-start(bf16[8,248,128]{2,1,0:T(8,128)(2,1)} %shard_map.47), calls=%async_computation | async-start | bytes 1015808 | tf_op jit(solution)/shard_map/all_to_all | solution.py:173
  66.3 0.0 copy-done.1
  66.3 10.0 %all-to-all-done = bf16[8,248,128]{2,1,0:T(8,128)(2,1)S(1)} async-done(((bf16[8,248,128]{2,1,0:T(8,128)(2,1)}), bf16[8,248,128]{2,1,0:T(8,128)(2,1)S(1)}, u32[]{:S(2)}, u32[]{:S(2)}) %all-to-all-start) | async-done | bytes 507936 | tf_op jit(solution)/shard_map/all_to_all | solution.py:173
  76.4 0.1 convert_reduce_fusion
  76.5 0.2 add_convert_fusion
  76.7 20.4 %all_to_all.15 = bf16[8,248,128]{2,1,0:T(8,128)(2,1)S(1)} all-to-all(bf16[8,248,128]{2,1,0:T(8,128)(2,1)S(1)} %add_convert_fusion), channel_id=1, replica_groups=mesh['x'=4,'core'=2,'u'=4,'v'=2,'hi'=2,'pair'=3,'duo'=2] {'x','core'}, dimensions={0} | all-to-all | bytes 1015808 | tf_op jit(solution)/shard_map/all_to_all | solution.py:177
  97.1 0.1 reduce_sum.22
  97.1 0.1 broadcast_in_dim.4
  97.2 20.0 %all_to_all.16.packed_ref = bf16[6,248,128]{2,1,0:T(8,128)(2,1)S(1)} all-to-all(bf16[6,248,128]{2,1,0:T(8,128)(2,1)S(1)} %broadcast_in_dim.4), channel_id=1, replica_groups=mesh['x'=4,'core'=2,'u'=4,'v'=2,'hi'=2,'pair'=3,'duo'=2] {'pair','duo'}, dimensions={0} | all-to-all | bytes 761856 | tf_op jit(solution)/shard_map/all_to_all | solution.py:18
  117.2 1.0 shard_map.48
  (8 shorter events, 0.1 us)
Async XLA Ops:
  0.0 1.6 %copy-start = (bf16[2,288,1728]{2,1,0:T(8,128)(2,1)S(1)}, bf16[2,288,1728]{2,1,0:T(8,128)(2,1)}, u32[]{:S(2)}) copy-start(bf16[2,288,1728]{2,1,0:T(8,128)(2,1)} %param.5) | copy-start | bytes 5971972
  3.4 6.5 %collective-permute-start.3 = (bf16[288,108]{1,0:T(8,128)(2,1)S(1)}, bf16[288,108]{1,0:T(8,128)(2,1)S(1)}, u32[]{:S(2)}, u32[]{:S(2)}) collective-permute-start(bf16[288,108]{1,0:T(8,128)(2,1)S(1)} %dynamic-slice_bitcast_fusion.1), channel_id=1, source_target_pairs={{0,1},{1,0},{2,3},{3,2},{4,5},{5,4},{6,7},{7,6},{8,9},{9,8},{10,11... | collective-permute-start | bytes 186632 | tf_op jit(solution)/shard_map/ppermute | solution.py:142
  10.0 17.5 %collective-permute-start.4 = (bf16[576,108]{1,0:T(8,128)(2,1)S(1)}, bf16[576,108]{1,0:T(8,128)(2,1)S(1)}, u32[]{:S(2)}, u32[]{:S(2)}) collective-permute-start(bf16[576,108]{1,0:T(8,128)(2,1)S(1)} %pad_maximum_fusion.2), channel_id=1, source_target_pairs={{0,6},{6,0},{1,7},{7,1},{2,8},{8,2},{3,9},{9,3},{4,10},{10,4},{5,1... | collective-permute-start | bytes 373256 | tf_op jit(solution)/shard_map/ppermute | solution.py:146
  24.7 14.4 %collective-permute-start = (bf16[2,384,128]{2,1,0:T(8,128)(2,1)S(1)}, bf16[2,384,128]{2,1,0:T(8,128)(2,1)S(1)}, u32[]{:S(2)}, u32[]{:S(2)}) collective-permute-start(bf16[2,384,128]{2,1,0:T(8,128)(2,1)S(1)} %dynamic-slice_bitcast_fusion), channel_id=1, source_target_pairs={{0,1},{1,0},{2,3},{3,2},{4,5},{5,4},{6,7},{7,6},{8,9},{9,8},{10,11... | collective-permute-start | bytes 589832 | tf_op jit(solution)/shard_map/ppermute | solution.py:136
  27.8 20.9 %collective-permute-start.5 = (bf16[576,216]{1,0:T(8,128)(2,1)S(1)}, bf16[576,216]{1,0:T(8,128)(2,1)S(1)}, u32[]{:S(2)}, u32[]{:S(2)}) collective-permute-start(bf16[576,216]{1,0:T(8,128)(2,1)S(1)} %pad_maximum_fusion.1), channel_id=1, source_target_pairs={{0,12},{12,0},{1,13},{13,1},{2,14},{14,2},{3,15},{15,3},{4,16},{16... | collective-permute-start | bytes 746504 | tf_op jit(solution)/shard_map/ppermute | solution.py:156
  39.2 12.2 %collective-permute-start.1 = (bf16[2,384,128]{2,1,0:T(8,128)(2,1)S(1)}, bf16[2,384,128]{2,1,0:T(8,128)(2,1)S(1)}, u32[]{:S(2)}, u32[]{:S(2)}) collective-permute-start(bf16[2,384,128]{2,1,0:T(8,128)(2,1)S(1)} %get-tuple-element.13), channel_id=1, source_target_pairs={{0,2},{1,3},{2,4},{3,5},{4,6},{5,7},{6,8},{7,9},{8,10},{9,11},{10,... | collective-permute-start | bytes 589832 | tf_op jit(solution)/shard_map/ppermute | solution.py:151
  41.5 14.4 %collective-permute-start.2 = (bf16[2,384,128]{2,1,0:T(8,128)(2,1)S(1)}, bf16[2,384,128]{2,1,0:T(8,128)(2,1)S(1)}, u32[]{:S(2)}, u32[]{:S(2)}) collective-permute-start(bf16[2,384,128]{2,1,0:T(8,128)(2,1)S(1)} %get-tuple-element.11), channel_id=1, source_target_pairs={{2,0},{3,1},{4,2},{5,3},{6,4},{7,5},{8,6},{9,7},{10,8},{11,9},{0,1... | collective-permute-start | bytes 589832 | tf_op jit(solution)/shard_map/ppermute | solution.py:152
  49.0 17.3 %copy-start.1 = (bf16[2,8]{1,0:T(2,128)(2,1)S(1)}, bf16[2,8]{1,0:T(2,128)(2,1)}, u32[]{:S(2)}) copy-start(bf16[2,8]{1,0:T(2,128)(2,1)} %param.7) | copy-start | bytes 100
  58.5 17.9 %all-to-all-start = ((bf16[8,248,128]{2,1,0:T(8,128)(2,1)}), bf16[8,248,128]{2,1,0:T(8,128)(2,1)S(1)}, u32[]{:S(2)}, u32[]{:S(2)}) async-start(bf16[8,248,128]{2,1,0:T(8,128)(2,1)} %shard_map.47), calls=%async_computation | async-start | bytes 1015808 | tf_op jit(solution)/shard_map/all_to_all | solution.py:173
where the time goes:
time: 119 us; the launch traced here: 118 us
  starting transfers between devices  42.7 us (36%)
  blocking collectives  40.4 us (34%)
  waiting for transfers between devices  25 us (21%)
  Pallas kernels  3.65 us (3%)
  local copies, waits for them, and re-layouts  3.04 us (3%)
  matrix products  1.83 us (2%)
  other arithmetic  1.28 us (1%)
    all_to_all x1, blocking collectives, body(): terms = lax.all_to_all(terms, ('x', 'core'), 0, 0, tiled=True)  20.4 us
    all_to_all x1, blocking collectives, spread(): lax.all_to_all(jnp.broadcast_to(block[None], (n, *block.shape)), axis, 0,...  20 us
    ppermute x1, starting transfers between devices, body(): other = lax.ppermute(own, 'hi', SWAP)  14.6 us
    all_to_all x1, waiting for transfers between devices, body(): part = lax.all_to_all(part, ('u', 'duo'), 0, 0, tiled=True)  10 us
    ppermute x1, waiting for transfers between devices, body(): taken = lax.ppermute(pick(windows, 1 - duo), 'duo', SWAP)  8.05 us
    all_to_all x1, starting transfers between devices, body(): part = lax.all_to_all(part, ('u', 'duo'), 0, 0, tiled=True)  7.8 us
    ppermute x1, starting transfers between devices, body(): above = lax.ppermute(pick(windows, down), Z, [(j, i) for i, j in turn])  7.14 us
    ppermute x1, starting transfers between devices, body(): near = lax.ppermute(odd, 'duo', SWAP)  4.81 us
  transfers between devices with their start and end apart: 7, of which 5 were waited for; matrix products, arithmetic and copies ran while one was open for 2% of the time, Pallas kernels for 0%

commit v1 on v0

--- a/solution.py
+++ b/solution.py
@@ -150,12 +150,13 @@
     turn = [(i, (i + DUO) % ring) for i in range(ring)]
     below = lax.ppermute(pick(windows, up), Z, turn)
     above = lax.ppermute(pick(windows, down), Z, [(j, i) for i, j in turn])
-    own = jnp.concatenate(
-        [jnp.where(hi == 0, own, other), jnp.where(hi == 0, other, own)], axis=1
+    beside = [lax.ppermute(own, "v", SWAP), lax.ppermute(other, "v", SWAP)]
+    ours, theirs = (
+        jnp.concatenate([jnp.where(hi == 0, a, b), jnp.where(hi == 0, b, a)], axis=1)
+        for a, b in ((own, other), beside)
     )
-    other = lax.ppermute(own, "v", SWAP)
     first = jnp.concatenate(
-        [jnp.where(v == 0, own, other), jnp.where(v == 0, other, own)], axis=1
+        [jnp.where(v == 0, ours, theirs), jnp.where(v == 0, theirs, ours)], axis=1
     ).reshape(DUO, share, depth)
 
     deep = fold_size(rows, share)

time: 119 us -> 119 us (level)
  waiting for transfers between devices: 25 us -> 22.8 us
  starting transfers between devices: 42.7 us -> 44.9 us
    ppermute x1 -> x2, starting transfers between devices: 3.21 us -> 5.27 us  [body(): beside = [lax.ppermute(own, 'v', SWAP), lax.ppermute(other, 'v', SWAP)]]
    ppermute x1, waiting for transfers between devices: 8.05 us -> 6.12 us  [body(): taken = lax.ppermute(pick(windows, 1 - duo), 'duo', SWAP)]
  transfers between devices with their start and end apart: 7 -> 8, of which waited for: 5 -> 5; matrix products, arithmetic and copies ran while one was open for 2% -> 2% of each run, Pallas kernels for 0% -> 0%
where the time goes in v1:
time: 119 us; the launch traced here: 118 us
  starting transfers between devices  44.9 us (38%)
  blocking collectives  40.5 us (34%)
  waiting for transfers between devices  22.8 us (19%)
  Pallas kernels  3.65 us (3%)
  local copies, waits for them, and re-layouts  3.04 us (3%)
  matrix products  1.83 us (2%)
    all_to_all x1, blocking collectives, body(): terms = lax.all_to_all(terms, ('x', 'core'), 0, 0, tiled=True)  20.3 us
    all_to_all x1, blocking collectives, spread(): lax.all_to_all(jnp.broadcast_to(block[None], (n, *block.shape)), axis, 0,...  20.2 us
    ppermute x1, starting transfers between devices, body(): other = lax.ppermute(own, 'hi', SWAP)  14.6 us
    all_to_all x1, waiting for transfers between devices, body(): part = lax.all_to_all(part, ('u', 'duo'), 0, 0, tiled=True)  10 us
    all_to_all x1, starting transfers between devices, body(): part = lax.all_to_all(part, ('u', 'duo'), 0, 0, tiled=True)  8.14 us
    ppermute x1, starting transfers between devices, body(): above = lax.ppermute(pick(windows, down), Z, [(j, i) for i, j in turn])  6.98 us
    ppermute x1, waiting for transfers between devices, body(): taken = lax.ppermute(pick(windows, 1 - duo), 'duo', SWAP)  6.12 us
    ppermute x2, starting transfers between devices, body(): beside = [lax.ppermute(own, 'v', SWAP), lax.ppermute(other, 'v', SWAP)]  5.27 us
  transfers between devices with their start and end apart: 8, of which 5 were waited for; matrix products, arithmetic and copies ran while one was open for 2% of the time, Pallas kernels for 0%

profile of v1, /device:TPU:1, one launch (start us, length us, event | category | flops | bytes accessed | tf_op | source)
XLA Modules:
  0.0 118.2 jit_solution(5283425180763664523)
XLA Ops:
  0.0 0.0 copy-start
  0.0 1.6 %copy-done = bf16[2,288,1728]{2,1,0:T(8,128)(2,1)S(1)} copy-done((bf16[2,288,1728]{2,1,0:T(8,128)(2,1)S(1)}, bf16[2,288,1728]{2,1,0:T(8,128)(2,1)}, u32[]{:S(2)}) %copy-start) | copy-done | bytes 1990680
  1.6 1.8 %convolution_convert_fusion = bf16[2,288,108]{2,1,0:T(8,128)(2,1)S(1)} fusion(bf16[2,288,1728]{2,1,0:T(8,128)(2,1)S(1)} %copy-done, bf16[2,108,1728]{2,0,1:T(2,128)(2,1)} %param.4), kind=kOutput, calls=%fused_computation | convolution fusion | flops 215053056 | bytes 2861568 | tf_op jit(solution)/shard_map/cil,cjl->cij/dot_general | solution.py:116
  3.4 4.8 %collective-permute-start.3 = (bf16[288,108]{1,0:T(8,128)(2,1)S(1)}, bf16[288,108]{1,0:T(8,128)(2,1)S(1)}, u32[]{:S(2)}, u32[]{:S(2)}) collective-permute-start(bf16[288,108]{1,0:T(8,128)(2,1)S(1)} %dynamic-slice_bitcast_fusion.1), channel_id=1, source_target_pairs={{0,1},{1,0},{2,3},{3,2},{4,5},{5,4},{6,7},{7,6},{8,9},{9,8},{10,11... | collective-permute-start | bytes 186632 | tf_op jit(solution)/shard_map/ppermute | solution.py:142
  8.3 1.3 %constant_dynamic-slice_fusion = (bf16[2,108,432]{2,1,0:T(8,128)(2,1)S(1)}, bf16[2,108,432]{2,1,0:T(8,128)(2,1)S(1)}) fusion(bf16[2,288,1728]{2,1,0:T(8,128)(2,1)} %param.6, s32[]{:T(128)S(6)} %min.8, s32[]{:T(128)S(6)} %select_n.103, s32[]{:T(128)S(6)} %min.7), kind=kLoop, calls=%fused_computation.36 | loop fusion | bytes 746508 | tf_op jit(solution)/shard_map/dynamic_slice | solution.py:127
  9.7 0.1 shard_map.46
  9.8 0.2 collective-permute-done.3
  10.0 14.6 %collective-permute-start.4 = (bf16[576,108]{1,0:T(8,128)(2,1)S(1)}, bf16[576,108]{1,0:T(8,128)(2,1)S(1)}, u32[]{:S(2)}, u32[]{:S(2)}) collective-permute-start(bf16[576,108]{1,0:T(8,128)(2,1)S(1)} %pad_maximum_fusion.3), channel_id=1, source_target_pairs={{0,6},{6,0},{1,7},{7,1},{2,8},{8,2},{3,9},{9,3},{4,10},{10,4},{5,1... | collective-permute-start | bytes 373256 | tf_op jit(solution)/shard_map/ppermute | solution.py:146
  24.7 2.8 %collective-permute-start = (bf16[2,384,128]{2,1,0:T(8,128)(2,1)S(1)}, bf16[2,384,128]{2,1,0:T(8,128)(2,1)S(1)}, u32[]{:S(2)}, u32[]{:S(2)}) collective-permute-start(bf16[2,384,128]{2,1,0:T(8,128)(2,1)S(1)} %dynamic-slice_bitcast_fusion), channel_id=1, source_target_pairs={{0,1},{1,0},{2,3},{3,2},{4,5},{5,4},{6,7},{7,6},{8,9},{9,8},{10,11... | collective-permute-start | bytes 589832 | tf_op jit(solution)/shard_map/ppermute | solution.py:136
  27.5 0.1 pad_add_fusion.where_ref
  27.6 3.2 %collective-permute-start.5 = (bf16[576,108]{1,0:T(8,128)(2,1)S(1)}, bf16[576,108]{1,0:T(8,128)(2,1)S(1)}, u32[]{:S(2)}, u32[]{:S(2)}) collective-permute-start(bf16[576,108]{1,0:T(8,128)(2,1)S(1)} %pad_maximum_fusion.3), channel_id=1, source_target_pairs={{0,12},{12,0},{1,13},{13,1},{2,14},{14,2},{3,15},{15,3},{4,16},{16... | collective-permute-start | bytes 373256 | tf_op jit(solution)/shard_map/ppermute | solution.py:153
  30.8 0.0 collective-permute-done.4
  30.8 2.1 %collective-permute-start.6 = (bf16[576,108]{1,0:T(8,128)(2,1)S(1)}, bf16[576,108]{1,0:T(8,128)(2,1)S(1)}, u32[]{:S(2)}, u32[]{:S(2)}) collective-permute-start(bf16[576,108]{1,0:T(8,128)(2,1)S(1)} %collective-permute-done.4), channel_id=1, source_target_pairs={{0,12},{12,0},{1,13},{13,1},{2,14},{14,2},{3,15},{15,3},{4,16},{16... | collective-permute-start | bytes 373256 | tf_op jit(solution)/shard_map/ppermute | solution.py:153
  32.9 0.1 broadcast_select_fusion.5
  32.9 6.1 %collective-permute-done = bf16[2,384,128]{2,1,0:T(8,128)(2,1)S(1)} collective-permute-done((bf16[2,384,128]{2,1,0:T(8,128)(2,1)S(1)}, bf16[2,384,128]{2,1,0:T(8,128)(2,1)S(1)}, u32[]{:S(2)}, u32[]{:S(2)}) %collective-permute-start) | collective-permute-done | bytes 196640 | tf_op jit(solution)/shard_map/ppermute | solution.py:136
  39.1 0.1 fusion.2
  39.2 2.4 %collective-permute-start.1 = (bf16[2,384,128]{2,1,0:T(8,128)(2,1)S(1)}, bf16[2,384,128]{2,1,0:T(8,128)(2,1)S(1)}, u32[]{:S(2)}, u32[]{:S(2)}) collective-permute-start(bf16[2,384,128]{2,1,0:T(8,128)(2,1)S(1)} %get-tuple-element.13), channel_id=1, source_target_pairs={{0,2},{1,3},{2,4},{3,5},{4,6},{5,7},{6,8},{7,9},{8,10},{9,11},{10,... | collective-permute-start | bytes 589832 | tf_op jit(solution)/shard_map/ppermute | solution.py:151
  41.5 7.0 %collective-permute-start.2 = (bf16[2,384,128]{2,1,0:T(8,128)(2,1)S(1)}, bf16[2,384,128]{2,1,0:T(8,128)(2,1)S(1)}, u32[]{:S(2)}, u32[]{:S(2)}) collective-permute-start(bf16[2,384,128]{2,1,0:T(8,128)(2,1)S(1)} %get-tuple-element.11), channel_id=1, source_target_pairs={{2,0},{3,1},{4,2},{5,3},{6,4},{7,5},{8,6},{9,7},{10,8},{11,9},{0,1... | collective-permute-start | bytes 589832 | tf_op jit(solution)/shard_map/ppermute | solution.py:152
  48.5 0.0 collective-permute-done.5
  48.5 0.0 collective-permute-done.6
  48.6 0.3 broadcast_select_fusion.1
  48.9 0.0 copy-start.1
  48.9 0.2 pad_maximum_fusion.first_ref
  49.1 2.1 %collective-permute-done.1.below_ref = bf16[2,384,128]{2,1,0:T(8,128)(2,1)S(1)} collective-permute-done((bf16[2,384,128]{2,1,0:T(8,128)(2,1)S(1)}, bf16[2,384,128]{2,1,0:T(8,128)(2,1)S(1)}, u32[]{:S(2)}, u32[]{:S(2)}) %collective-permute-start.1) | collective-permute-done | bytes 196640 | tf_op jit(solution)/shard_map/ppermute | solution.py:151
  51.2 4.3 %collective-permute-done.2.above_ref = bf16[2,384,128]{2,1,0:T(8,128)(2,1)S(1)} collective-permute-done((bf16[2,384,128]{2,1,0:T(8,128)(2,1)S(1)}, bf16[2,384,128]{2,1,0:T(8,128)(2,1)S(1)}, u32[]{:S(2)}, u32[]{:S(2)}) %collective-permute-start.2) | collective-permute-done | bytes 196640 | tf_op jit(solution)/shard_map/ppermute | solution.py:152
  55.5 2.6 %shard_map.47 = bf16[8,248,128]{2,1,0:T(8,128)(2,1)} custom-call(s32[4]{0:T(128)S(1)} %pad_add_fusion.where_ref, bf16[2,384,128]{2,1,0:T(8,128)(2,1)S(1)} %get-tuple-element.12.here_ref, bf16[2,384,128]{2,1,0:T(8,128)(2,1)S(1)} %collective-permute-done.1.below_ref, bf16[2,384,128]{2,1,0:T(8,128)(2,1)S(1)} %collective-permute-done.2.above_ref, ...), custom_call_target="tpu_custom_call" | custom-call | tf_op jit(solution)/shard_map/pallas_call | solution.py:163
  58.1 8.1 %all-to-all-start = ((bf16[8,248,128]{2,1,0:T(8,128)(2,1)}), bf16[8,248,128]{2,1,0:T(8,128)(2,1)S(1)}, u32[]{:S(2)}, u32[]{:S(2)}) async-start(bf16[8,248,128]{2,1,0:T(8,128)(2,1)} %shard_map.47), calls=%async_computation | async-start | bytes 1015808 | tf_op jit(solution)/shard_map/all_to_all | solution.py:174
  66.2 0.0 copy-done.1
  66.2 10.0 %all-to-all-done = bf16[8,248,128]{2,1,0:T(8,128)(2,1)S(1)} async-done(((bf16[8,248,128]{2,1,0:T(8,128)(2,1)}), bf16[8,248,128]{2,1,0:T(8,128)(2,1)S(1)}, u32[]{:S(2)}, u32[]{:S(2)}) %all-to-all-start) | async-done | bytes 507936 | tf_op jit(solution)/shard_map/all_to_all | solution.py:174
  76.3 0.1 convert_reduce_fusion
  76.4 0.2 add_convert_fusion
  76.6 20.3 %all_to_all.15 = bf16[8,248,128]{2,1,0:T(8,128)(2,1)S(1)} all-to-all(bf16[8,248,128]{2,1,0:T(8,128)(2,1)S(1)} %add_convert_fusion), channel_id=1, replica_groups=mesh['x'=4,'core'=2,'u'=4,'v'=2,'hi'=2,'pair'=3,'duo'=2] {'x','core'}, dimensions={0} | all-to-all | bytes 1015808 | tf_op jit(solution)/shard_map/all_to_all | solution.py:178
  96.9 0.1 reduce_sum.22
  97.0 0.1 broadcast_in_dim.4
  97.0 20.2 %all_to_all.16.packed_ref = bf16[6,248,128]{2,1,0:T(8,128)(2,1)S(1)} all-to-all(bf16[6,248,128]{2,1,0:T(8,128)(2,1)S(1)} %broadcast_in_dim.4), channel_id=1, replica_groups=mesh['x'=4,'core'=2,'u'=4,'v'=2,'hi'=2,'pair'=3,'duo'=2] {'pair','duo'}, dimensions={0} | all-to-all | bytes 761856 | tf_op jit(solution)/shard_map/all_to_all | solution.py:18
  117.2 1.0 shard_map.48
  (9 shorter events, 0.2 us)
Async XLA Ops:
  0.0 1.6 %copy-start = (bf16[2,288,1728]{2,1,0:T(8,128)(2,1)S(1)}, bf16[2,288,1728]{2,1,0:T(8,128)(2,1)}, u32[]{:S(2)}) copy-start(bf16[2,288,1728]{2,1,0:T(8,128)(2,1)} %param.5) | copy-start | bytes 5971972
  3.4 6.5 %collective-permute-start.3 = (bf16[288,108]{1,0:T(8,128)(2,1)S(1)}, bf16[288,108]{1,0:T(8,128)(2,1)S(1)}, u32[]{:S(2)}, u32[]{:S(2)}) collective-permute-start(bf16[288,108]{1,0:T(8,128)(2,1)S(1)} %dynamic-slice_bitcast_fusion.1), channel_id=1, source_target_pairs={{0,1},{1,0},{2,3},{3,2},{4,5},{5,4},{6,7},{7,6},{8,9},{9,8},{10,11... | collective-permute-start | bytes 186632 | tf_op jit(solution)/shard_map/ppermute | solution.py:142
  10.0 20.7 %collective-permute-start.4 = (bf16[576,108]{1,0:T(8,128)(2,1)S(1)}, bf16[576,108]{1,0:T(8,128)(2,1)S(1)}, u32[]{:S(2)}, u32[]{:S(2)}) collective-permute-start(bf16[576,108]{1,0:T(8,128)(2,1)S(1)} %pad_maximum_fusion.3), channel_id=1, source_target_pairs={{0,6},{6,0},{1,7},{7,1},{2,8},{8,2},{3,9},{9,3},{4,10},{10,4},{5,1... | collective-permute-start | bytes 373256 | tf_op jit(solution)/shard_map/ppermute | solution.py:146
  24.7 14.4 %collective-permute-start = (bf16[2,384,128]{2,1,0:T(8,128)(2,1)S(1)}, bf16[2,384,128]{2,1,0:T(8,128)(2,1)S(1)}, u32[]{:S(2)}, u32[]{:S(2)}) collective-permute-start(bf16[2,384,128]{2,1,0:T(8,128)(2,1)S(1)} %dynamic-slice_bitcast_fusion), channel_id=1, source_target_pairs={{0,1},{1,0},{2,3},{3,2},{4,5},{5,4},{6,7},{7,6},{8,9},{9,8},{10,11... | collective-permute-start | bytes 589832 | tf_op jit(solution)/shard_map/ppermute | solution.py:136
  27.6 21.0 %collective-permute-start.5 = (bf16[576,108]{1,0:T(8,128)(2,1)S(1)}, bf16[576,108]{1,0:T(8,128)(2,1)S(1)}, u32[]{:S(2)}, u32[]{:S(2)}) collective-permute-start(bf16[576,108]{1,0:T(8,128)(2,1)S(1)} %pad_maximum_fusion.3), channel_id=1, source_target_pairs={{0,12},{12,0},{1,13},{13,1},{2,14},{14,2},{3,15},{15,3},{4,16},{16... | collective-permute-start | bytes 373256 | tf_op jit(solution)/shard_map/ppermute | solution.py:153
  30.8 17.8 %collective-permute-start.6 = (bf16[576,108]{1,0:T(8,128)(2,1)S(1)}, bf16[576,108]{1,0:T(8,128)(2,1)S(1)}, u32[]{:S(2)}, u32[]{:S(2)}) collective-permute-start(bf16[576,108]{1,0:T(8,128)(2,1)S(1)} %collective-permute-done.4), channel_id=1, source_target_pairs={{0,12},{12,0},{1,13},{13,1},{2,14},{14,2},{3,15},{15,3},{4,16},{16... | collective-permute-start | bytes 373256 | tf_op jit(solution)/shard_map/ppermute | solution.py:153
  39.2 12.0 %collective-permute-start.1 = (bf16[2,384,128]{2,1,0:T(8,128)(2,1)S(1)}, bf16[2,384,128]{2,1,0:T(8,128)(2,1)S(1)}, u32[]{:S(2)}, u32[]{:S(2)}) collective-permute-start(bf16[2,384,128]{2,1,0:T(8,128)(2,1)S(1)} %get-tuple-element.13), channel_id=1, source_target_pairs={{0,2},{1,3},{2,4},{3,5},{4,6},{5,7},{6,8},{7,9},{8,10},{9,11},{10,... | collective-permute-start | bytes 589832 | tf_op jit(solution)/shard_map/ppermute | solution.py:151
  41.5 13.9 %collective-permute-start.2 = (bf16[2,384,128]{2,1,0:T(8,128)(2,1)S(1)}, bf16[2,384,128]{2,1,0:T(8,128)(2,1)S(1)}, u32[]{:S(2)}, u32[]{:S(2)}) collective-permute-start(bf16[2,384,128]{2,1,0:T(8,128)(2,1)S(1)} %get-tuple-element.11), channel_id=1, source_target_pairs={{2,0},{3,1},{4,2},{5,3},{6,4},{7,5},{8,6},{9,7},{10,8},{11,9},{0,1... | collective-permute-start | bytes 589832 | tf_op jit(solution)/shard_map/ppermute | solution.py:152
  48.9 17.3 %copy-start.1 = (bf16[2,8]{1,0:T(2,128)(2,1)S(1)}, bf16[2,8]{1,0:T(2,128)(2,1)}, u32[]{:S(2)}) copy-start(bf16[2,8]{1,0:T(2,128)(2,1)} %param.7) | copy-start | bytes 100
  58.1 18.2 %all-to-all-start = ((bf16[8,248,128]{2,1,0:T(8,128)(2,1)}), bf16[8,248,128]{2,1,0:T(8,128)(2,1)S(1)}, u32[]{:S(2)}, u32[]{:S(2)}) async-start(bf16[8,248,128]{2,1,0:T(8,128)(2,1)} %shard_map.47), calls=%async_computation | async-start | bytes 1015808 | tf_op jit(solution)/shard_map/all_to_all | solution.py:174

commit v2 on v1

--- a/solution.py
+++ b/solution.py
@@ -6,7 +6,7 @@
 from jax.sharding import Mesh, PartitionSpec as P
 
 
-U, V, HI, PAIRS, DUO = 4, 2, 2, 3, 2
+X, CORE, U, V, HI, PAIRS, DUO = 4, 2, 4, 2, 2, 3, 2
 LANES = 128
 SWAP = [(0, 1), (1, 0)]
 REP = ("pair", "duo")
@@ -95,13 +95,17 @@
                 second_ref[block], first_ref[duo], (((1,), (1,)), ((), ())),
                 preferred_element_type=F32,
             )
-            out_ref[block * DUO + duo] = folded(got, out_ref.shape[1]).astype(BF16)
+            out_ref[duo * U + block] = folded(got, out_ref.shape[1]).astype(BF16)
 
 
 def unpack(packed_ref, out_ref):
     n_rep, rows = packed_ref.shape[0], out_ref.shape[0]
     share = out_ref.shape[1] // n_rep
-    columns = [unfolded(packed_ref[rep].astype(F32), rows, share) for rep in range(n_rep)]
+    columns = [
+        unfolded(packed_ref[duo * PAIRS + pair].astype(F32), rows, share)
+        for pair in range(PAIRS)
+        for duo in range(DUO)
+    ]
     out_ref[...] = jnp.concatenate(columns, axis=1).astype(BF16)
 
 
@@ -171,13 +175,14 @@
         ],
         compiler_params=params,
     )(jnp.stack(where).astype(jnp.int32), pick(windows, hi), below, above, first)
-    part = lax.all_to_all(part, ("u", "duo"), 0, 0, tiled=True)
-    part = part.reshape(U, DUO, deep, LANES).astype(F32).sum(0)
-    weights = environment.astype(F32)[:, :, None, None]
+    part = lax.all_to_all(part, ("duo", "u"), 0, 0, tiled=True)
+    part = part.reshape(DUO, U, deep, LANES).astype(F32).sum(1)
+    weights = environment.astype(F32).reshape(slices, X, CORE).swapaxes(1, 2)
+    weights = weights.reshape(slices, X * CORE, 1, 1)
     terms = sum(weights[c] * part[c] for c in range(slices)).astype(BF16)
-    terms = lax.all_to_all(terms, ("x", "core"), 0, 0, tiled=True)
+    terms = lax.all_to_all(terms, ("core", "x"), 0, 0, tiled=True)
     closed = jnp.sum(terms.astype(F32), 0).astype(BF16)
-    whole = spread(closed, REP, n_rep)
+    whole = spread(closed, REP[::-1], n_rep)
     return pl.pallas_call(
         unpack,
         out_shape=jax.ShapeDtypeStruct((rows, width), BF16),
@@ -189,7 +194,7 @@
 
 def solution(mesh):
     fine = Mesh(
-        mesh.devices.reshape(4, 2, U, V, HI, PAIRS, DUO),
+        mesh.devices.reshape(X, CORE, U, V, HI, PAIRS, DUO),
         ("x", "core", "u", "v", "hi", *REP),
     )
     cuts, stem = ("x", "core"), ("u", "v", "hi")

time: 119 us -> 118 us (level)
  the two profiles are of different devices: /device:TPU:1 before, /device:TPU:8 now
where the time goes in v2:
time: 118 us; the launch traced here: 117 us
  starting transfers between devices  44.2 us (37%)
  blocking collectives  34 us (29%)
  waiting for transfers between devices  28.4 us (24%)
  Pallas kernels  3.64 us (3%)
  local copies, waits for them, and re-layouts  3.5 us (3%)
  matrix products  1.82 us (2%)
    all_to_all x1, blocking collectives, spread(): lax.all_to_all(jnp.broadcast_to(block[None], (n, *block.shape)), axis, 0,...  20.6 us
    all_to_all x1, waiting for transfers between devices, body(): part = lax.all_to_all(part, ('duo', 'u'), 0, 0, tiled=True)  15 us
    ppermute x1, starting transfers between devices, body(): other = lax.ppermute(own, 'hi', SWAP)  14.8 us
    all_to_all x1, blocking collectives, body(): terms = lax.all_to_all(terms, ('core', 'x'), 0, 0, tiled=True)  13.4 us
    all_to_all x1, starting transfers between devices, body(): part = lax.all_to_all(part, ('duo', 'u'), 0, 0, tiled=True)  8.71 us
    ppermute x1, starting transfers between devices, body(): above = lax.ppermute(pick(windows, down), Z, [(j, i) for i, j in turn])  5.35 us
    ppermute x2, starting transfers between devices, body(): beside = [lax.ppermute(own, 'v', SWAP), lax.ppermute(other, 'v', SWAP)]  5.08 us
    ppermute x1, waiting for transfers between devices, body(): above = lax.ppermute(pick(windows, down), Z, [(j, i) for i, j in turn])  5.06 us
  transfers between devices with their start and end apart: 8, of which 6 were waited for; matrix products, arithmetic and copies ran while one was open for 2% of the time, Pallas kernels for 0%

profile of v2, /device:TPU:8, one launch (start us, length us, event | category | flops | bytes accessed | tf_op | source)
XLA Modules:
  0.0 117.0 jit_solution(10381803967962356082)
XLA Ops:
  0.0 0.0 copy-start
  0.0 1.6 %copy-done = bf16[2,288,1728]{2,1,0:T(8,128)(2,1)S(1)} copy-done((bf16[2,288,1728]{2,1,0:T(8,128)(2,1)S(1)}, bf16[2,288,1728]{2,1,0:T(8,128)(2,1)}, u32[]{:S(2)}) %copy-start) | copy-done | bytes 1990680
  1.6 1.8 %convolution_convert_fusion = bf16[2,288,108]{2,1,0:T(8,128)(2,1)S(1)} fusion(bf16[2,288,1728]{2,1,0:T(8,128)(2,1)S(1)} %copy-done, bf16[2,108,1728]{2,0,1:T(2,128)(2,1)} %param.4), kind=kOutput, calls=%fused_computation | convolution fusion | flops 215053056 | bytes 2861568 | tf_op jit(solution)/shard_map/cil,cjl->cij/dot_general | solution.py:120
  3.4 4.3 %collective-permute-start.3 = (bf16[288,108]{1,0:T(8,128)(2,1)S(1)}, bf16[288,108]{1,0:T(8,128)(2,1)S(1)}, u32[]{:S(2)}, u32[]{:S(2)}) collective-permute-start(bf16[288,108]{1,0:T(8,128)(2,1)S(1)} %dynamic-slice_bitcast_fusion.1), channel_id=1, source_target_pairs={{0,1},{1,0},{2,3},{3,2},{4,5},{5,4},{6,7},{7,6},{8,9},{9,8},{10,11... | collective-permute-start | bytes 186632 | tf_op jit(solution)/shard_map/ppermute | solution.py:146
  7.8 1.4 %constant_dynamic-slice_fusion = (bf16[2,108,432]{2,1,0:T(8,128)(2,1)S(1)}, bf16[2,108,432]{2,1,0:T(8,128)(2,1)S(1)}) fusion(bf16[2,288,1728]{2,1,0:T(8,128)(2,1)} %param.6, s32[]{:T(128)S(6)} %min.8, s32[]{:T(128)S(6)} %select_n.103, s32[]{:T(128)S(6)} %min.7), kind=kLoop, calls=%fused_computation.36 | loop fusion | bytes 746508 | tf_op jit(solution)/shard_map/dynamic_slice | solution.py:131
  9.2 0.1 shard_map.46
  9.3 0.8 collective-permute-done.3
  10.1 14.8 %collective-permute-start.4 = (bf16[576,108]{1,0:T(8,128)(2,1)S(1)}, bf16[576,108]{1,0:T(8,128)(2,1)S(1)}, u32[]{:S(2)}, u32[]{:S(2)}) collective-permute-start(bf16[576,108]{1,0:T(8,128)(2,1)S(1)} %pad_maximum_fusion.3), channel_id=1, source_target_pairs={{0,6},{6,0},{1,7},{7,1},{2,8},{8,2},{3,9},{9,3},{4,10},{10,4},{5,1... | collective-permute-start | bytes 373256 | tf_op jit(solution)/shard_map/ppermute | solution.py:150
  25.0 3.3 %collective-permute-start = (bf16[2,384,128]{2,1,0:T(8,128)(2,1)S(1)}, bf16[2,384,128]{2,1,0:T(8,128)(2,1)S(1)}, u32[]{:S(2)}, u32[]{:S(2)}) collective-permute-start(bf16[2,384,128]{2,1,0:T(8,128)(2,1)S(1)} %dynamic-slice_bitcast_fusion), channel_id=1, source_target_pairs={{0,1},{1,0},{2,3},{3,2},{4,5},{5,4},{6,7},{7,6},{8,9},{9,8},{10,11... | collective-permute-start | bytes 589832 | tf_op jit(solution)/shard_map/ppermute | solution.py:140
  28.4 0.1 pad_add_fusion.where_ref
  28.5 2.3 %collective-permute-start.5 = (bf16[576,108]{1,0:T(8,128)(2,1)S(1)}, bf16[576,108]{1,0:T(8,128)(2,1)S(1)}, u32[]{:S(2)}, u32[]{:S(2)}) collective-permute-start(bf16[576,108]{1,0:T(8,128)(2,1)S(1)} %pad_maximum_fusion.3), channel_id=1, source_target_pairs={{0,12},{12,0},{1,13},{13,1},{2,14},{14,2},{3,15},{15,3},{4,16},{16... | collective-permute-start | bytes 373256 | tf_op jit(solution)/shard_map/ppermute | solution.py:157
  30.8 2.7 %collective-permute-done.4 = bf16[576,108]{1,0:T(8,128)(2,1)S(1)} collective-permute-done((bf16[576,108]{1,0:T(8,128)(2,1)S(1)}, bf16[576,108]{1,0:T(8,128)(2,1)S(1)}, u32[]{:S(2)}, u32[]{:S(2)}) %collective-permute-start.4) | collective-permute-done | bytes 124448 | tf_op jit(solution)/shard_map/ppermute | solution.py:150
  33.5 2.7 %collective-permute-start.6 = (bf16[576,108]{1,0:T(8,128)(2,1)S(1)}, bf16[576,108]{1,0:T(8,128)(2,1)S(1)}, u32[]{:S(2)}, u32[]{:S(2)}) collective-permute-start(bf16[576,108]{1,0:T(8,128)(2,1)S(1)} %collective-permute-done.4), channel_id=1, source_target_pairs={{0,12},{12,0},{1,13},{13,1},{2,14},{14,2},{3,15},{15,3},{4,16},{16... | collective-permute-start | bytes 373256 | tf_op jit(solution)/shard_map/ppermute | solution.py:157
  36.3 0.1 broadcast_select_fusion.5
  36.3 3.2 %collective-permute-done = bf16[2,384,128]{2,1,0:T(8,128)(2,1)S(1)} collective-permute-done((bf16[2,384,128]{2,1,0:T(8,128)(2,1)S(1)}, bf16[2,384,128]{2,1,0:T(8,128)(2,1)S(1)}, u32[]{:S(2)}, u32[]{:S(2)}) %collective-permute-start) | collective-permute-done | bytes 196640 | tf_op jit(solution)/shard_map/ppermute | solution.py:140
  39.6 0.1 fusion.2
  39.7 2.6 %collective-permute-start.1 = (bf16[2,384,128]{2,1,0:T(8,128)(2,1)S(1)}, bf16[2,384,128]{2,1,0:T(8,128)(2,1)S(1)}, u32[]{:S(2)}, u32[]{:S(2)}) collective-permute-start(bf16[2,384,128]{2,1,0:T(8,128)(2,1)S(1)} %get-tuple-element.13), channel_id=1, source_target_pairs={{0,2},{1,3},{2,4},{3,5},{4,6},{5,7},{6,8},{7,9},{8,10},{9,11},{10,... | collective-permute-start | bytes 589832 | tf_op jit(solution)/shard_map/ppermute | solution.py:155
  42.3 5.3 %collective-permute-start.2 = (bf16[2,384,128]{2,1,0:T(8,128)(2,1)S(1)}, bf16[2,384,128]{2,1,0:T(8,128)(2,1)S(1)}, u32[]{:S(2)}, u32[]{:S(2)}) collective-permute-start(bf16[2,384,128]{2,1,0:T(8,128)(2,1)S(1)} %get-tuple-element.11), channel_id=1, source_target_pairs={{2,0},{3,1},{4,2},{5,3},{6,4},{7,5},{8,6},{9,7},{10,8},{11,9},{0,1... | collective-permute-start | bytes 589832 | tf_op jit(solution)/shard_map/ppermute | solution.py:156
  47.6 0.0 collective-permute-done.5
  47.6 0.0 collective-permute-done.6
  47.7 0.3 broadcast_select_fusion.1
  48.0 0.0 copy-start.1
  48.0 0.2 pad_maximum_fusion.first_ref
  48.2 1.6 %collective-permute-done.1.below_ref = bf16[2,384,128]{2,1,0:T(8,128)(2,1)S(1)} collective-permute-done((bf16[2,384,128]{2,1,0:T(8,128)(2,1)S(1)}, bf16[2,384,128]{2,1,0:T(8,128)(2,1)S(1)}, u32[]{:S(2)}, u32[]{:S(2)}) %collective-permute-start.1) | collective-permute-done | bytes 196640 | tf_op jit(solution)/shard_map/ppermute | solution.py:155
  49.8 5.1 %collective-permute-done.2.above_ref = bf16[2,384,128]{2,1,0:T(8,128)(2,1)S(1)} collective-permute-done((bf16[2,384,128]{2,1,0:T(8,128)(2,1)S(1)}, bf16[2,384,128]{2,1,0:T(8,128)(2,1)S(1)}, u32[]{:S(2)}, u32[]{:S(2)}) %collective-permute-start.2) | collective-permute-done | bytes 196640 | tf_op jit(solution)/shard_map/ppermute | solution.py:156
  54.9 2.6 %shard_map.47 = bf16[8,248,128]{2,1,0:T(8,128)(2,1)} custom-call(s32[4]{0:T(128)S(1)} %pad_add_fusion.where_ref, bf16[2,384,128]{2,1,0:T(8,128)(2,1)S(1)} %get-tuple-element.12.here_ref, bf16[2,384,128]{2,1,0:T(8,128)(2,1)S(1)} %collective-permute-done.1.below_ref, bf16[2,384,128]{2,1,0:T(8,128)(2,1)S(1)} %collective-permute-done.2.above_ref, ...), custom_call_target="tpu_custom_call" | custom-call | tf_op jit(solution)/shard_map/pallas_call | solution.py:167
  57.4 8.7 %all-to-all-start = ((bf16[8,248,128]{2,1,0:T(8,128)(2,1)}), bf16[8,248,128]{2,1,0:T(8,128)(2,1)S(1)}, u32[]{:S(2)}, u32[]{:S(2)}) async-start(bf16[8,248,128]{2,1,0:T(8,128)(2,1)} %shard_map.47), calls=%async_computation | async-start | bytes 1015808 | tf_op jit(solution)/shard_map/all_to_all | solution.py:178
  66.1 0.0 copy-done.1
  66.2 0.1 reshape.28
  66.2 0.1 copy.13
  66.3 0.1 mul.70
  66.4 0.1 copy.16
  66.5 0.1 mul.85
  66.6 15.0 %all-to-all-done = bf16[8,248,128]{2,1,0:T(8,128)(2,1)S(1)} async-done(((bf16[8,248,128]{2,1,0:T(8,128)(2,1)}), bf16[8,248,128]{2,1,0:T(8,128)(2,1)S(1)}, u32[]{:S(2)}, u32[]{:S(2)}) %all-to-all-start) | async-done | bytes 507936 | tf_op jit(solution)/shard_map/all_to_all | solution.py:178
  81.6 0.1 convert_reduce_fusion
  81.7 0.2 add_convert_fusion
  81.9 13.4 %all_to_all.15 = bf16[8,248,128]{2,1,0:T(8,128)(2,1)S(1)} all-to-all(bf16[8,248,128]{2,1,0:T(8,128)(2,1)S(1)} %add_convert_fusion), channel_id=1, replica_groups=mesh['x'=4,'core'=2,'u'=4,'v'=2,'hi'=2,'pair'=3,'duo'=2] {'core','x'}, dimensions={0} | all-to-all | bytes 1015808 | tf_op jit(solution)/shard_map/all_to_all | solution.py:183
  95.3 0.1 reduce_sum.22
  95.4 0.1 broadcast_in_dim.4
  95.4 20.6 %all_to_all.16.packed_ref = bf16[6,248,128]{2,1,0:T(8,128)(2,1)S(1)} all-to-all(bf16[6,248,128]{2,1,0:T(8,128)(2,1)S(1)} %broadcast_in_dim.4), channel_id=1, replica_groups=mesh['x'=4,'core'=2,'u'=4,'v'=2,'hi'=2,'pair'=3,'duo'=2] {'duo','pair'}, dimensions={0} | all-to-all | bytes 761856 | tf_op jit(solution)/shard_map/all_to_all | solution.py:18
  116.0 1.0 shard_map.48
  (8 shorter events, 0.2 us)
Async XLA Ops:
  0.0 1.6 %copy-start = (bf16[2,288,1728]{2,1,0:T(8,128)(2,1)S(1)}, bf16[2,288,1728]{2,1,0:T(8,128)(2,1)}, u32[]{:S(2)}) copy-start(bf16[2,288,1728]{2,1,0:T(8,128)(2,1)} %param.5) | copy-start | bytes 5971972
  3.4 6.6 %collective-permute-start.3 = (bf16[288,108]{1,0:T(8,128)(2,1)S(1)}, bf16[288,108]{1,0:T(8,128)(2,1)S(1)}, u32[]{:S(2)}, u32[]{:S(2)}) collective-permute-start(bf16[288,108]{1,0:T(8,128)(2,1)S(1)} %dynamic-slice_bitcast_fusion.1), channel_id=1, source_target_pairs={{0,1},{1,0},{2,3},{3,2},{4,5},{5,4},{6,7},{7,6},{8,9},{9,8},{10,11... | collective-permute-start | bytes 186632 | tf_op jit(solution)/shard_map/ppermute | solution.py:146
  10.1 23.4 %collective-permute-start.4 = (bf16[576,108]{1,0:T(8,128)(2,1)S(1)}, bf16[576,108]{1,0:T(8,128)(2,1)S(1)}, u32[]{:S(2)}, u32[]{:S(2)}) collective-permute-start(bf16[576,108]{1,0:T(8,128)(2,1)S(1)} %pad_maximum_fusion.3), channel_id=1, source_target_pairs={{0,6},{6,0},{1,7},{7,1},{2,8},{8,2},{3,9},{9,3},{4,10},{10,4},{5,1... | collective-permute-start | bytes 373256 | tf_op jit(solution)/shard_map/ppermute | solution.py:150
  25.0 14.6 %collective-permute-start = (bf16[2,384,128]{2,1,0:T(8,128)(2,1)S(1)}, bf16[2,384,128]{2,1,0:T(8,128)(2,1)S(1)}, u32[]{:S(2)}, u32[]{:S(2)}) collective-permute-start(bf16[2,384,128]{2,1,0:T(8,128)(2,1)S(1)} %dynamic-slice_bitcast_fusion), channel_id=1, source_target_pairs={{0,1},{1,0},{2,3},{3,2},{4,5},{5,4},{6,7},{7,6},{8,9},{9,8},{10,11... | collective-permute-start | bytes 589832 | tf_op jit(solution)/shard_map/ppermute | solution.py:140
  28.5 19.2 %collective-permute-start.5 = (bf16[576,108]{1,0:T(8,128)(2,1)S(1)}, bf16[576,108]{1,0:T(8,128)(2,1)S(1)}, u32[]{:S(2)}, u32[]{:S(2)}) collective-permute-start(bf16[576,108]{1,0:T(8,128)(2,1)S(1)} %pad_maximum_fusion.3), channel_id=1, source_target_pairs={{0,12},{12,0},{1,13},{13,1},{2,14},{14,2},{3,15},{15,3},{4,16},{16... | collective-permute-start | bytes 373256 | tf_op jit(solution)/shard_map/ppermute | solution.py:157
  33.5 14.1 %collective-permute-start.6 = (bf16[576,108]{1,0:T(8,128)(2,1)S(1)}, bf16[576,108]{1,0:T(8,128)(2,1)S(1)}, u32[]{:S(2)}, u32[]{:S(2)}) collective-permute-start(bf16[576,108]{1,0:T(8,128)(2,1)S(1)} %collective-permute-done.4), channel_id=1, source_target_pairs={{0,12},{12,0},{1,13},{13,1},{2,14},{14,2},{3,15},{15,3},{4,16},{16... | collective-permute-start | bytes 373256 | tf_op jit(solution)/shard_map/ppermute | solution.py:157
  39.7 10.2 %collective-permute-start.1 = (bf16[2,384,128]{2,1,0:T(8,128)(2,1)S(1)}, bf16[2,384,128]{2,1,0:T(8,128)(2,1)S(1)}, u32[]{:S(2)}, u32[]{:S(2)}) collective-permute-start(bf16[2,384,128]{2,1,0:T(8,128)(2,1)S(1)} %get-tuple-element.13), channel_id=1, source_target_pairs={{0,2},{1,3},{2,4},{3,5},{4,6},{5,7},{6,8},{7,9},{8,10},{9,11},{10,... | collective-permute-start | bytes 589832 | tf_op jit(solution)/shard_map/ppermute | solution.py:155
  42.3 12.6 %collective-permute-start.2 = (bf16[2,384,128]{2,1,0:T(8,128)(2,1)S(1)}, bf16[2,384,128]{2,1,0:T(8,128)(2,1)S(1)}, u32[]{:S(2)}, u32[]{:S(2)}) collective-permute-start(bf16[2,384,128]{2,1,0:T(8,128)(2,1)S(1)} %get-tuple-element.11), channel_id=1, source_target_pairs={{2,0},{3,1},{4,2},{5,3},{6,4},{7,5},{8,6},{9,7},{10,8},{11,9},{0,1... | collective-permute-start | bytes 589832 | tf_op jit(solution)/shard_map/ppermute | solution.py:156
  48.0 18.2 %copy-start.1 = (bf16[2,8]{1,0:T(2,128)(2,1)S(1)}, bf16[2,8]{1,0:T(2,128)(2,1)}, u32[]{:S(2)}) copy-start(bf16[2,8]{1,0:T(2,128)(2,1)} %param.7) | copy-start | bytes 100
  57.4 24.2 %all-to-all-start = ((bf16[8,248,128]{2,1,0:T(8,128)(2,1)}), bf16[8,248,128]{2,1,0:T(8,128)(2,1)S(1)}, u32[]{:S(2)}, u32[]{:S(2)}) async-start(bf16[8,248,128]{2,1,0:T(8,128)(2,1)} %shard_map.47), calls=%async_computation | async-start | bytes 1015808 | tf_op jit(solution)/shard_map/all_to_all | solution.py:178

commit v3 on v2

--- a/solution.py
+++ b/solution.py
@@ -65,12 +65,11 @@
     return -(-(lanes // LANES * rows + rows // (LANES // (lanes % LANES))) // 8) * 8
 
 
-def pack(*refs):
-    out_ref = refs[-1]
-    for side in range(HI):
-        for duo in range(DUO):
-            packed = folded(refs[side][duo].astype(F32), out_ref.shape[2])
-            out_ref[duo, side] = packed.astype(BF16)
+def pack(duo_ref, low_ref, high_ref, kept_ref, given_ref):
+    for side, ref in enumerate((low_ref, high_ref)):
+        for out_ref, duo in ((kept_ref, duo_ref[0]), (given_ref, 1 - duo_ref[0])):
+            packed = folded(ref[duo].astype(F32), out_ref.shape[1])
+            out_ref[side] = packed.astype(BF16)
 
 
 def multiply(where_ref, here_ref, below_ref, above_ref, first_ref, out_ref, window_ref, second_ref):
@@ -129,15 +128,15 @@
         block = lax.div(share * rep + (V * HI - 1) * rows - rows * owner, V * HI * rows)
         at = jnp.clip(rows * (owner + V * HI * block) - share * rep, 0, share - rows)
         windows.append(lax.dynamic_slice(site_second, (0, at, depth * u), (slices, rows, depth)))
-    windows = pl.pallas_call(
+    half = jax.ShapeDtypeStruct((HI, fold_size(rows, depth), LANES), BF16)
+    kept, given = pl.pallas_call(
         pack,
-        out_shape=jax.ShapeDtypeStruct((DUO, HI, fold_size(rows, depth), LANES), BF16),
-        in_specs=[vmem, vmem],
-        out_specs=vmem,
+        out_shape=(half, half),
+        in_specs=[pl.BlockSpec(memory_space=pltpu.SMEM), vmem, vmem],
+        out_specs=(vmem, vmem),
         compiler_params=params,
-    )(*windows)
-    kept = pick(windows, duo)
-    taken = lax.ppermute(pick(windows, 1 - duo), "duo", SWAP)
+    )(duo[None].astype(jnp.int32), *windows)
+    taken = lax.ppermute(given, "duo", SWAP)
     windows = jnp.stack(
         [jnp.where(duo == 0, kept, taken), jnp.where(duo == 0, taken, kept)], axis=1
     )

time: 118 us -> 117 us (level)
  the two profiles are of different devices: /device:TPU:8 before, /device:TPU:2 now
where the time goes in v3:
time: 117 us
  starting transfers between devices  45.2 us (39%)
  blocking collectives  33.4 us (29%)
  waiting for transfers between devices  27.5 us (24%)
  Pallas kernels  3.65 us (3%)
  local copies, waits for them, and re-layouts  3.46 us (3%)
  matrix products  1.83 us (2%)
    all_to_all x1, blocking collectives, spread(): lax.all_to_all(jnp.broadcast_to(block[None], (n, *block.shape)), axis, 0,...  20.4 us
    ppermute x1, starting transfers between devices, body(): other = lax.ppermute(own, 'hi', SWAP)  14.8 us
    all_to_all x1, waiting for transfers between devices, body(): part = lax.all_to_all(part, ('duo', 'u'), 0, 0, tiled=True)  14.7 us
    all_to_all x1, blocking collectives, body(): terms = lax.all_to_all(terms, ('core', 'x'), 0, 0, tiled=True)  13 us
    all_to_all x1, starting transfers between devices, body(): part = lax.all_to_all(part, ('duo', 'u'), 0, 0, tiled=True)  7.54 us
    ppermute x2, starting transfers between devices, body(): beside = [lax.ppermute(own, 'v', SWAP), lax.ppermute(other, 'v', SWAP)]  6.52 us
    ppermute x1, starting transfers between devices, body(): above = lax.ppermute(pick(windows, down), Z, [(j, i) for i, j in turn])  5.91 us
    ppermute x1, waiting for transfers between devices, body(): above = lax.ppermute(pick(windows, down), Z, [(j, i) for i, j in turn])  4.91 us
  transfers between devices with their start and end apart: 8, of which 5 were waited for; matrix products, arithmetic and copies ran while one was open for 2% of the time, Pallas kernels for 0%

profile of v3, /device:TPU:2, one launch (start us, length us, event | category | flops | bytes accessed | tf_op | source)
XLA Modules:
  0.0 116.5 jit_solution(10977829239487517295)
XLA Ops:
  0.0 0.0 copy-start
  0.0 1.6 %copy-done = bf16[2,288,1728]{2,1,0:T(8,128)(2,1)S(1)} copy-done((bf16[2,288,1728]{2,1,0:T(8,128)(2,1)S(1)}, bf16[2,288,1728]{2,1,0:T(8,128)(2,1)}, u32[]{:S(2)}) %copy-start) | copy-done | bytes 1990680
  1.6 1.8 %convolution_convert_fusion = bf16[2,288,108]{2,1,0:T(8,128)(2,1)S(1)} fusion(bf16[2,288,1728]{2,1,0:T(8,128)(2,1)S(1)} %copy-done, bf16[2,108,1728]{2,0,1:T(2,128)(2,1)} %param.4), kind=kOutput, calls=%fused_computation | convolution fusion | flops 215053056 | bytes 2861568 | tf_op jit(solution)/shard_map/cil,cjl->cij/dot_general | solution.py:119
  3.4 4.3 %collective-permute-start.3 = (bf16[288,108]{1,0:T(8,128)(2,1)S(1)}, bf16[288,108]{1,0:T(8,128)(2,1)S(1)}, u32[]{:S(2)}, u32[]{:S(2)}) collective-permute-start(bf16[288,108]{1,0:T(8,128)(2,1)S(1)} %dynamic-slice_bitcast_fusion), channel_id=1, source_target_pairs={{0,1},{1,0},{2,3},{3,2},{4,5},{5,4},{6,7},{7,6},{8,9},{9,8},{10,11... | collective-permute-start | bytes 186632 | tf_op jit(solution)/shard_map/ppermute | solution.py:145
  7.8 2.3 %collective-permute-done.3 = bf16[288,108]{1,0:T(8,128)(2,1)S(1)} collective-permute-done((bf16[288,108]{1,0:T(8,128)(2,1)S(1)}, bf16[288,108]{1,0:T(8,128)(2,1)S(1)}, u32[]{:S(2)}, u32[]{:S(2)}) %collective-permute-start.3) | collective-permute-done | bytes 62240 | tf_op jit(solution)/shard_map/ppermute | solution.py:145
  10.1 14.8 %collective-permute-start.4 = (bf16[576,108]{1,0:T(8,128)(2,1)S(1)}, bf16[576,108]{1,0:T(8,128)(2,1)S(1)}, u32[]{:S(2)}, u32[]{:S(2)}) collective-permute-start(bf16[576,108]{1,0:T(8,128)(2,1)S(1)} %pad_maximum_fusion.3), channel_id=1, source_target_pairs={{0,6},{6,0},{1,7},{7,1},{2,8},{8,2},{3,9},{9,3},{4,10},{10,4},{5,1... | collective-permute-start | bytes 373256 | tf_op jit(solution)/shard_map/ppermute | solution.py:149
  24.9 1.3 %constant_dynamic-slice_fusion = (bf16[2,108,432]{2,1,0:T(8,128)(2,1)S(1)}, bf16[2,108,432]{2,1,0:T(8,128)(2,1)S(1)}) fusion(bf16[2,288,1728]{2,1,0:T(8,128)(2,1)} %param.6, s32[]{:T(128)S(6)} %min.8, s32[]{:T(128)S(6)} %select_n.101, s32[]{:T(128)S(6)} %min.7), kind=kLoop, calls=%fused_computation.33 | loop fusion | bytes 746508 | tf_op jit(solution)/shard_map/dynamic_slice | solution.py:130
  26.3 0.1 shard_map.46
  26.4 3.3 %collective-permute-start = (bf16[2,384,128]{2,1,0:T(8,128)(2,1)S(1)}, bf16[2,384,128]{2,1,0:T(8,128)(2,1)S(1)}, u32[]{:S(2)}, u32[]{:S(2)}) collective-permute-start(bf16[2,384,128]{2,1,0:T(8,128)(2,1)S(1)} %get-tuple-element.8), channel_id=1, source_target_pairs={{0,1},{1,0},{2,3},{3,2},{4,5},{5,4},{6,7},{7,6},{8,9},{9,8},{10,11... | collective-permute-start | bytes 589832 | tf_op jit(solution)/shard_map/ppermute | solution.py:139
  29.8 0.1 pad_add_fusion.where_ref
  29.9 3.5 %collective-permute-start.5 = (bf16[576,108]{1,0:T(8,128)(2,1)S(1)}, bf16[576,108]{1,0:T(8,128)(2,1)S(1)}, u32[]{:S(2)}, u32[]{:S(2)}) collective-permute-start(bf16[576,108]{1,0:T(8,128)(2,1)S(1)} %pad_maximum_fusion.3), channel_id=1, source_target_pairs={{0,12},{12,0},{1,13},{13,1},{2,14},{14,2},{3,15},{15,3},{4,16},{16... | collective-permute-start | bytes 373256 | tf_op jit(solution)/shard_map/ppermute | solution.py:156
  33.4 0.0 collective-permute-done.4
  33.4 3.0 %collective-permute-start.6 = (bf16[576,108]{1,0:T(8,128)(2,1)S(1)}, bf16[576,108]{1,0:T(8,128)(2,1)S(1)}, u32[]{:S(2)}, u32[]{:S(2)}) collective-permute-start(bf16[576,108]{1,0:T(8,128)(2,1)S(1)} %collective-permute-done.4), channel_id=1, source_target_pairs={{0,12},{12,0},{1,13},{13,1},{2,14},{14,2},{3,15},{15,3},{4,16},{16... | collective-permute-start | bytes 373256 | tf_op jit(solution)/shard_map/ppermute | solution.py:156
  36.4 0.1 broadcast_select_fusion.5
  36.5 3.0 %collective-permute-done = bf16[2,384,128]{2,1,0:T(8,128)(2,1)S(1)} collective-permute-done((bf16[2,384,128]{2,1,0:T(8,128)(2,1)S(1)}, bf16[2,384,128]{2,1,0:T(8,128)(2,1)S(1)}, u32[]{:S(2)}, u32[]{:S(2)}) %collective-permute-start) | collective-permute-done | bytes 196640 | tf_op jit(solution)/shard_map/ppermute | solution.py:139
  39.6 0.1 fusion.2
  39.7 2.8 %collective-permute-start.1 = (bf16[2,384,128]{2,1,0:T(8,128)(2,1)S(1)}, bf16[2,384,128]{2,1,0:T(8,128)(2,1)S(1)}, u32[]{:S(2)}, u32[]{:S(2)}) collective-permute-start(bf16[2,384,128]{2,1,0:T(8,128)(2,1)S(1)} %get-tuple-element.15), channel_id=1, source_target_pairs={{0,2},{1,3},{2,4},{3,5},{4,6},{5,7},{6,8},{7,9},{8,10},{9,11},{10,... | collective-permute-start | bytes 589832 | tf_op jit(solution)/shard_map/ppermute | solution.py:154
  42.4 5.9 %collective-permute-start.2 = (bf16[2,384,128]{2,1,0:T(8,128)(2,1)S(1)}, bf16[2,384,128]{2,1,0:T(8,128)(2,1)S(1)}, u32[]{:S(2)}, u32[]{:S(2)}) collective-permute-start(bf16[2,384,128]{2,1,0:T(8,128)(2,1)S(1)} %get-tuple-element.13), channel_id=1, source_target_pairs={{2,0},{3,1},{4,2},{5,3},{6,4},{7,5},{8,6},{9,7},{10,8},{11,9},{0,1... | collective-permute-start | bytes 589832 | tf_op jit(solution)/shard_map/ppermute | solution.py:155
  48.4 0.0 collective-permute-done.5
  48.4 0.0 collective-permute-done.6
  48.4 0.3 broadcast_select_fusion.1
  48.7 0.0 copy-start.1
  48.7 0.2 pad_maximum_fusion.first_ref
  48.9 2.6 %collective-permute-done.1.below_ref = bf16[2,384,128]{2,1,0:T(8,128)(2,1)S(1)} collective-permute-done((bf16[2,384,128]{2,1,0:T(8,128)(2,1)S(1)}, bf16[2,384,128]{2,1,0:T(8,128)(2,1)S(1)}, u32[]{:S(2)}, u32[]{:S(2)}) %collective-permute-start.1) | collective-permute-done | bytes 196640 | tf_op jit(solution)/shard_map/ppermute | solution.py:154
  51.5 4.9 %collective-permute-done.2.above_ref = bf16[2,384,128]{2,1,0:T(8,128)(2,1)S(1)} collective-permute-done((bf16[2,384,128]{2,1,0:T(8,128)(2,1)S(1)}, bf16[2,384,128]{2,1,0:T(8,128)(2,1)S(1)}, u32[]{:S(2)}, u32[]{:S(2)}) %collective-permute-start.2) | collective-permute-done | bytes 196640 | tf_op jit(solution)/shard_map/ppermute | solution.py:155
  56.4 2.6 %shard_map.47 = bf16[8,248,128]{2,1,0:T(8,128)(2,1)} custom-call(s32[4]{0:T(128)S(1)} %pad_add_fusion.where_ref, bf16[2,384,128]{2,1,0:T(8,128)(2,1)S(1)} %get-tuple-element.14.here_ref, bf16[2,384,128]{2,1,0:T(8,128)(2,1)S(1)} %collective-permute-done.1.below_ref, bf16[2,384,128]{2,1,0:T(8,128)(2,1)S(1)} %collective-permute-done.2.above_ref, ...), custom_call_target="tpu_custom_call" | custom-call | tf_op jit(solution)/shard_map/pallas_call | solution.py:166
  59.0 7.5 %all-to-all-start = ((bf16[8,248,128]{2,1,0:T(8,128)(2,1)}), bf16[8,248,128]{2,1,0:T(8,128)(2,1)S(1)}, u32[]{:S(2)}, u32[]{:S(2)}) async-start(bf16[8,248,128]{2,1,0:T(8,128)(2,1)} %shard_map.47), calls=%async_computation | async-start | bytes 1015808 | tf_op jit(solution)/shard_map/all_to_all | solution.py:177
  66.5 0.0 copy-done.1
  66.5 0.1 reshape.28
  66.6 0.1 copy.11
  66.7 0.1 mul.70
  66.8 0.1 copy.13
  66.9 0.1 mul.85
  67.0 14.7 %all-to-all-done = bf16[8,248,128]{2,1,0:T(8,128)(2,1)S(1)} async-done(((bf16[8,248,128]{2,1,0:T(8,128)(2,1)}), bf16[8,248,128]{2,1,0:T(8,128)(2,1)S(1)}, u32[]{:S(2)}, u32[]{:S(2)}) %all-to-all-start) | async-done | bytes 507936 | tf_op jit(solution)/shard_map/all_to_all | solution.py:177
  81.7 0.1 convert_reduce_fusion
  81.8 0.2 add_convert_fusion
  82.0 13.0 %all_to_all.15 = bf16[8,248,128]{2,1,0:T(8,128)(2,1)S(1)} all-to-all(bf16[8,248,128]{2,1,0:T(8,128)(2,1)S(1)} %add_convert_fusion), channel_id=1, replica_groups=mesh['x'=4,'core'=2,'u'=4,'v'=2,'hi'=2,'pair'=3,'duo'=2] {'core','x'}, dimensions={0} | all-to-all | bytes 1015808 | tf_op jit(solution)/shard_map/all_to_all | solution.py:182
  95.0 0.1 reduce_sum.22
  95.1 0.1 broadcast_in_dim.13
  95.1 20.4 %all_to_all.16.packed_ref = bf16[6,248,128]{2,1,0:T(8,128)(2,1)S(1)} all-to-all(bf16[6,248,128]{2,1,0:T(8,128)(2,1)S(1)} %broadcast_in_dim.13), channel_id=1, replica_groups=mesh['x'=4,'core'=2,'u'=4,'v'=2,'hi'=2,'pair'=3,'duo'=2] {'duo','pair'}, dimensions={0} | all-to-all | bytes 761856 | tf_op jit(solution)/shard_map/all_to_all | solution.py:18
  115.5 1.0 shard_map.48
  (7 shorter events, 0.1 us)
Async XLA Ops:
  0.0 1.6 %copy-start = (bf16[2,288,1728]{2,1,0:T(8,128)(2,1)S(1)}, bf16[2,288,1728]{2,1,0:T(8,128)(2,1)}, u32[]{:S(2)}) copy-start(bf16[2,288,1728]{2,1,0:T(8,128)(2,1)} %param.5) | copy-start | bytes 5971972
  3.4 6.6 %collective-permute-start.3 = (bf16[288,108]{1,0:T(8,128)(2,1)S(1)}, bf16[288,108]{1,0:T(8,128)(2,1)S(1)}, u32[]{:S(2)}, u32[]{:S(2)}) collective-permute-start(bf16[288,108]{1,0:T(8,128)(2,1)S(1)} %dynamic-slice_bitcast_fusion), channel_id=1, source_target_pairs={{0,1},{1,0},{2,3},{3,2},{4,5},{5,4},{6,7},{7,6},{8,9},{9,8},{10,11... | collective-permute-start | bytes 186632 | tf_op jit(solution)/shard_map/ppermute | solution.py:145
  10.1 23.3 %collective-permute-start.4 = (bf16[576,108]{1,0:T(8,128)(2,1)S(1)}, bf16[576,108]{1,0:T(8,128)(2,1)S(1)}, u32[]{:S(2)}, u32[]{:S(2)}) collective-permute-start(bf16[576,108]{1,0:T(8,128)(2,1)S(1)} %pad_maximum_fusion.3), channel_id=1, source_target_pairs={{0,6},{6,0},{1,7},{7,1},{2,8},{8,2},{3,9},{9,3},{4,10},{10,4},{5,1... | collective-permute-start | bytes 373256 | tf_op jit(solution)/shard_map/ppermute | solution.py:149
  26.4 13.2 %collective-permute-start = (bf16[2,384,128]{2,1,0:T(8,128)(2,1)S(1)}, bf16[2,384,128]{2,1,0:T(8,128)(2,1)S(1)}, u32[]{:S(2)}, u32[]{:S(2)}) collective-permute-start(bf16[2,384,128]{2,1,0:T(8,128)(2,1)S(1)} %get-tuple-element.8), channel_id=1, source_target_pairs={{0,1},{1,0},{2,3},{3,2},{4,5},{5,4},{6,7},{7,6},{8,9},{9,8},{10,11... | collective-permute-start | bytes 589832 | tf_op jit(solution)/shard_map/ppermute | solution.py:139
  29.9 18.5 %collective-permute-start.5 = (bf16[576,108]{1,0:T(8,128)(2,1)S(1)}, bf16[576,108]{1,0:T(8,128)(2,1)S(1)}, u32[]{:S(2)}, u32[]{:S(2)}) collective-permute-start(bf16[576,108]{1,0:T(8,128)(2,1)S(1)} %pad_maximum_fusion.3), channel_id=1, source_target_pairs={{0,12},{12,0},{1,13},{13,1},{2,14},{14,2},{3,15},{15,3},{4,16},{16... | collective-permute-start | bytes 373256 | tf_op jit(solution)/shard_map/ppermute | solution.py:156
  33.4 15.0 %collective-permute-start.6 = (bf16[576,108]{1,0:T(8,128)(2,1)S(1)}, bf16[576,108]{1,0:T(8,128)(2,1)S(1)}, u32[]{:S(2)}, u32[]{:S(2)}) collective-permute-start(bf16[576,108]{1,0:T(8,128)(2,1)S(1)} %collective-permute-done.4), channel_id=1, source_target_pairs={{0,12},{12,0},{1,13},{13,1},{2,14},{14,2},{3,15},{15,3},{4,16},{16... | collective-permute-start | bytes 373256 | tf_op jit(solution)/shard_map/ppermute | solution.py:156
  39.7 11.8 %collective-permute-start.1 = (bf16[2,384,128]{2,1,0:T(8,128)(2,1)S(1)}, bf16[2,384,128]{2,1,0:T(8,128)(2,1)S(1)}, u32[]{:S(2)}, u32[]{:S(2)}) collective-permute-start(bf16[2,384,128]{2,1,0:T(8,128)(2,1)S(1)} %get-tuple-element.15), channel_id=1, source_target_pairs={{0,2},{1,3},{2,4},{3,5},{4,6},{5,7},{6,8},{7,9},{8,10},{9,11},{10,... | collective-permute-start | bytes 589832 | tf_op jit(solution)/shard_map/ppermute | solution.py:154
  42.4 14.0 %collective-permute-start.2 = (bf16[2,384,128]{2,1,0:T(8,128)(2,1)S(1)}, bf16[2,384,128]{2,1,0:T(8,128)(2,1)S(1)}, u32[]{:S(2)}, u32[]{:S(2)}) collective-permute-start(bf16[2,384,128]{2,1,0:T(8,128)(2,1)S(1)} %get-tuple-element.13), channel_id=1, source_target_pairs={{2,0},{3,1},{4,2},{5,3},{6,4},{7,5},{8,6},{9,7},{10,8},{11,9},{0,1... | collective-permute-start | bytes 589832 | tf_op jit(solution)/shard_map/ppermute | solution.py:155
  48.7 17.8 %copy-start.1 = (bf16[2,8]{1,0:T(2,128)(2,1)S(1)}, bf16[2,8]{1,0:T(2,128)(2,1)}, u32[]{:S(2)}) copy-start(bf16[2,8]{1,0:T(2,128)(2,1)} %param.7) | copy-start | bytes 100
  59.0 22.7 %all-to-all-start = ((bf16[8,248,128]{2,1,0:T(8,128)(2,1)}), bf16[8,248,128]{2,1,0:T(8,128)(2,1)S(1)}, u32[]{:S(2)}, u32[]{:S(2)}) async-start(bf16[8,248,128]{2,1,0:T(8,128)(2,1)} %shard_map.47), calls=%async_computation | async-start | bytes 1015808 | tf_op jit(solution)/shard_map/all_to_all | solution.py:177

commit v4 on v3

--- a/solution.py
+++ b/solution.py
@@ -72,10 +72,10 @@
             out_ref[side] = packed.astype(BF16)
 
 
-def multiply(where_ref, here_ref, below_ref, above_ref, first_ref, out_ref, window_ref, second_ref):
+def assemble(where_ref, here_ref, below_ref, above_ref, second_ref, window_ref):
     n_rep = window_ref.shape[0]
     rows, depth = second_ref.shape[1:]
-    share = first_ref.shape[1]
+    share = U * depth // n_rep
     for place, ref in enumerate((here_ref, below_ref, above_ref)):
         for duo in range(DUO):
             window_ref[DUO * where_ref[1 + place] + duo] = unfolded(
@@ -88,6 +88,8 @@
             for block, row, rep, held, count in pieces_of(owner, rows, share, n_rep):
                 second_ref[block, row : row + count] = window_ref[rep, held : held + count]
 
+
+def multiply(second_ref, first_ref, out_ref):
     for block in range(second_ref.shape[0]):
         for duo in range(DUO):
             got = lax.dot_general(
@@ -163,17 +165,21 @@
     ).reshape(DUO, share, depth)
 
     deep = fold_size(rows, share)
+    second = pl.pallas_call(
+        assemble,
+        out_shape=jax.ShapeDtypeStruct((U, rows, depth), BF16),
+        in_specs=[pl.BlockSpec(memory_space=pltpu.SMEM), vmem, vmem, vmem],
+        out_specs=vmem,
+        scratch_shapes=[pltpu.VMEM((n_rep, rows, depth), BF16)],
+        compiler_params=params,
+    )(jnp.stack(where).astype(jnp.int32), pick(windows, hi), below, above)
     part = pl.pallas_call(
         multiply,
         out_shape=jax.ShapeDtypeStruct((U * DUO, deep, LANES), BF16),
-        in_specs=[pl.BlockSpec(memory_space=pltpu.SMEM), vmem, vmem, vmem, vmem],
+        in_specs=[vmem, vmem],
         out_specs=vmem,
-        scratch_shapes=[
-            pltpu.VMEM((n_rep, rows, depth), BF16),
-            pltpu.VMEM((U, rows, depth), BF16),
-        ],
-        compiler_params=params,
-    )(jnp.stack(where).astype(jnp.int32), pick(windows, hi), below, above, first)
+        compiler_params=params,
+    )(second, first)
     part = lax.all_to_all(part, ("duo", "u"), 0, 0, tiled=True)
     part = part.reshape(DUO, U, deep, LANES).astype(F32).sum(1)
     weights = environment.astype(F32).reshape(slices, X, CORE).swapaxes(1, 2)

time: 117 us -> 117 us (level)
  no operation moved by 1% of the time
where the time goes in v4:
time: 117 us
  starting transfers between devices  45.2 us (39%)
  blocking collectives  33.4 us (29%)
  waiting for transfers between devices  27.5 us (24%)
  Pallas kernels  3.66 us (3%)
  local copies, waits for them, and re-layouts  3.46 us (3%)
  matrix products  1.83 us (2%)
    all_to_all x1, blocking collectives, spread(): lax.all_to_all(jnp.broadcast_to(block[None], (n, *block.shape)), axis, 0,...  20.4 us
    ppermute x1, starting transfers between devices, body(): other = lax.ppermute(own, 'hi', SWAP)  14.8 us
    all_to_all x1, waiting for transfers between devices, body(): part = lax.all_to_all(part, ('duo', 'u'), 0, 0, tiled=True)  14.8 us
    all_to_all x1, blocking collectives, body(): terms = lax.all_to_all(terms, ('core', 'x'), 0, 0, tiled=True)  12.9 us
    all_to_all x1, starting transfers between devices, body(): part = lax.all_to_all(part, ('duo', 'u'), 0, 0, tiled=True)  7.54 us
    ppermute x2, starting transfers between devices, body(): beside = [lax.ppermute(own, 'v', SWAP), lax.ppermute(other, 'v', SWAP)]  6.52 us
    ppermute x1, starting transfers between devices, body(): above = lax.ppermute(pick(windows, down), Z, [(j, i) for i, j in turn])  5.91 us
    ppermute x1, waiting for transfers between devices, body(): above = lax.ppermute(pick(windows, down), Z, [(j, i) for i, j in turn])  4.91 us
  transfers between devices with their start and end apart: 8, of which 5 were waited for; matrix products, arithmetic and copies ran while one was open for 2% of the time, Pallas kernels for 0%

profile of v4, /device:TPU:2, one launch (start us, length us, event | category | flops | bytes accessed | tf_op | source)
XLA Modules:
  0.0 116.5 jit_solution(5355442755519260883)
XLA Ops:
  0.0 0.0 copy-start
  0.0 1.6 %copy-done = bf16[2,288,1728]{2,1,0:T(8,128)(2,1)S(1)} copy-done((bf16[2,288,1728]{2,1,0:T(8,128)(2,1)S(1)}, bf16[2,288,1728]{2,1,0:T(8,128)(2,1)}, u32[]{:S(2)}) %copy-start) | copy-done | bytes 1990680
  1.6 1.8 %convolution_convert_fusion = bf16[2,288,108]{2,1,0:T(8,128)(2,1)S(1)} fusion(bf16[2,288,1728]{2,1,0:T(8,128)(2,1)S(1)} %copy-done, bf16[2,108,1728]{2,0,1:T(2,128)(2,1)} %param.4), kind=kOutput, calls=%fused_computation | convolution fusion | flops 215053056 | bytes 2861568 | tf_op jit(solution)/shard_map/cil,cjl->cij/dot_general | solution.py:121
  3.4 4.3 %collective-permute-start.3 = (bf16[288,108]{1,0:T(8,128)(2,1)S(1)}, bf16[288,108]{1,0:T(8,128)(2,1)S(1)}, u32[]{:S(2)}, u32[]{:S(2)}) collective-permute-start(bf16[288,108]{1,0:T(8,128)(2,1)S(1)} %dynamic-slice_bitcast_fusion), channel_id=1, source_target_pairs={{0,1},{1,0},{2,3},{3,2},{4,5},{5,4},{6,7},{7,6},{8,9},{9,8},{10,11... | collective-permute-start | bytes 186632 | tf_op jit(solution)/shard_map/ppermute | solution.py:147
  7.8 2.3 %collective-permute-done.3 = bf16[288,108]{1,0:T(8,128)(2,1)S(1)} collective-permute-done((bf16[288,108]{1,0:T(8,128)(2,1)S(1)}, bf16[288,108]{1,0:T(8,128)(2,1)S(1)}, u32[]{:S(2)}, u32[]{:S(2)}) %collective-permute-start.3) | collective-permute-done | bytes 62240 | tf_op jit(solution)/shard_map/ppermute | solution.py:147
  10.1 14.8 %collective-permute-start.4 = (bf16[576,108]{1,0:T(8,128)(2,1)S(1)}, bf16[576,108]{1,0:T(8,128)(2,1)S(1)}, u32[]{:S(2)}, u32[]{:S(2)}) collective-permute-start(bf16[576,108]{1,0:T(8,128)(2,1)S(1)} %pad_maximum_fusion.3), channel_id=1, source_target_pairs={{0,6},{6,0},{1,7},{7,1},{2,8},{8,2},{3,9},{9,3},{4,10},{10,4},{5,1... | collective-permute-start | bytes 373256 | tf_op jit(solution)/shard_map/ppermute | solution.py:151
  24.9 1.3 %constant_dynamic-slice_fusion = (bf16[2,108,432]{2,1,0:T(8,128)(2,1)S(1)}, bf16[2,108,432]{2,1,0:T(8,128)(2,1)S(1)}) fusion(bf16[2,288,1728]{2,1,0:T(8,128)(2,1)} %param.6, s32[]{:T(128)S(6)} %min.8, s32[]{:T(128)S(6)} %select_n.101, s32[]{:T(128)S(6)} %min.7), kind=kLoop, calls=%fused_computation.33 | loop fusion | bytes 746508 | tf_op jit(solution)/shard_map/dynamic_slice | solution.py:132
  26.3 0.1 shard_map.46
  26.4 3.3 %collective-permute-start = (bf16[2,384,128]{2,1,0:T(8,128)(2,1)S(1)}, bf16[2,384,128]{2,1,0:T(8,128)(2,1)S(1)}, u32[]{:S(2)}, u32[]{:S(2)}) collective-permute-start(bf16[2,384,128]{2,1,0:T(8,128)(2,1)S(1)} %get-tuple-element.8), channel_id=1, source_target_pairs={{0,1},{1,0},{2,3},{3,2},{4,5},{5,4},{6,7},{7,6},{8,9},{9,8},{10,11... | collective-permute-start | bytes 589832 | tf_op jit(solution)/shard_map/ppermute | solution.py:141
  29.8 0.1 pad_add_fusion.where_ref
  29.9 3.5 %collective-permute-start.5 = (bf16[576,108]{1,0:T(8,128)(2,1)S(1)}, bf16[576,108]{1,0:T(8,128)(2,1)S(1)}, u32[]{:S(2)}, u32[]{:S(2)}) collective-permute-start(bf16[576,108]{1,0:T(8,128)(2,1)S(1)} %pad_maximum_fusion.3), channel_id=1, source_target_pairs={{0,12},{12,0},{1,13},{13,1},{2,14},{14,2},{3,15},{15,3},{4,16},{16... | collective-permute-start | bytes 373256 | tf_op jit(solution)/shard_map/ppermute | solution.py:158
  33.4 0.0 collective-permute-done.4
  33.4 3.0 %collective-permute-start.6 = (bf16[576,108]{1,0:T(8,128)(2,1)S(1)}, bf16[576,108]{1,0:T(8,128)(2,1)S(1)}, u32[]{:S(2)}, u32[]{:S(2)}) collective-permute-start(bf16[576,108]{1,0:T(8,128)(2,1)S(1)} %collective-permute-done.4), channel_id=1, source_target_pairs={{0,12},{12,0},{1,13},{13,1},{2,14},{14,2},{3,15},{15,3},{4,16},{16... | collective-permute-start | bytes 373256 | tf_op jit(solution)/shard_map/ppermute | solution.py:158
  36.4 0.1 broadcast_select_fusion.5
  36.5 3.0 %collective-permute-done = bf16[2,384,128]{2,1,0:T(8,128)(2,1)S(1)} collective-permute-done((bf16[2,384,128]{2,1,0:T(8,128)(2,1)S(1)}, bf16[2,384,128]{2,1,0:T(8,128)(2,1)S(1)}, u32[]{:S(2)}, u32[]{:S(2)}) %collective-permute-start) | collective-permute-done | bytes 196640 | tf_op jit(solution)/shard_map/ppermute | solution.py:141
  39.6 0.1 fusion.2
  39.7 2.8 %collective-permute-start.1 = (bf16[2,384,128]{2,1,0:T(8,128)(2,1)S(1)}, bf16[2,384,128]{2,1,0:T(8,128)(2,1)S(1)}, u32[]{:S(2)}, u32[]{:S(2)}) collective-permute-start(bf16[2,384,128]{2,1,0:T(8,128)(2,1)S(1)} %get-tuple-element.15), channel_id=1, source_target_pairs={{0,2},{1,3},{2,4},{3,5},{4,6},{5,7},{6,8},{7,9},{8,10},{9,11},{10,... | collective-permute-start | bytes 589832 | tf_op jit(solution)/shard_map/ppermute | solution.py:156
  42.4 5.9 %collective-permute-start.2 = (bf16[2,384,128]{2,1,0:T(8,128)(2,1)S(1)}, bf16[2,384,128]{2,1,0:T(8,128)(2,1)S(1)}, u32[]{:S(2)}, u32[]{:S(2)}) collective-permute-start(bf16[2,384,128]{2,1,0:T(8,128)(2,1)S(1)} %get-tuple-element.13), channel_id=1, source_target_pairs={{2,0},{3,1},{4,2},{5,3},{6,4},{7,5},{8,6},{9,7},{10,8},{11,9},{0,1... | collective-permute-start | bytes 589832 | tf_op jit(solution)/shard_map/ppermute | solution.py:157
  48.4 0.0 collective-permute-done.5
  48.4 0.0 collective-permute-done.6
  48.4 0.3 broadcast_select_fusion.1
  48.7 0.2 pad_maximum_fusion.first_ref
  48.9 0.0 copy-start.1
  48.9 2.6 %collective-permute-done.1.below_ref = bf16[2,384,128]{2,1,0:T(8,128)(2,1)S(1)} collective-permute-done((bf16[2,384,128]{2,1,0:T(8,128)(2,1)S(1)}, bf16[2,384,128]{2,1,0:T(8,128)(2,1)S(1)}, u32[]{:S(2)}, u32[]{:S(2)}) %collective-permute-start.1) | collective-permute-done | bytes 196640 | tf_op jit(solution)/shard_map/ppermute | solution.py:156
  51.5 4.9 %collective-permute-done.2.above_ref = bf16[2,384,128]{2,1,0:T(8,128)(2,1)S(1)} collective-permute-done((bf16[2,384,128]{2,1,0:T(8,128)(2,1)S(1)}, bf16[2,384,128]{2,1,0:T(8,128)(2,1)S(1)}, u32[]{:S(2)}, u32[]{:S(2)}) %collective-permute-start.2) | collective-permute-done | bytes 196640 | tf_op jit(solution)/shard_map/ppermute | solution.py:157
  56.4 0.7 shard_map.47.second_ref
  57.1 1.8 %shard_map.48 = bf16[8,248,128]{2,1,0:T(8,128)(2,1)} custom-call(bf16[4,108,432]{2,1,0:T(8,128)(2,1)S(1)} %shard_map.47.second_ref, bf16[2,288,432]{2,1,0:T(8,128)(2,1)S(1)} %pad_maximum_fusion.first_ref), custom_call_target="tpu_custom_call" | custom-call | tf_op jit(solution)/shard_map/pallas_call | solution.py:176
  59.0 7.5 %all-to-all-start = ((bf16[8,248,128]{2,1,0:T(8,128)(2,1)}), bf16[8,248,128]{2,1,0:T(8,128)(2,1)S(1)}, u32[]{:S(2)}, u32[]{:S(2)}) async-start(bf16[8,248,128]{2,1,0:T(8,128)(2,1)} %shard_map.48), calls=%async_computation | async-start | bytes 1015808 | tf_op jit(solution)/shard_map/all_to_all | solution.py:183
  66.5 0.0 copy-done.1
  66.5 0.1 reshape.28
  66.6 0.1 copy.11
  66.7 0.1 mul.70
  66.8 0.1 copy.13
  66.9 0.1 mul.85
  67.0 14.8 %all-to-all-done = bf16[8,248,128]{2,1,0:T(8,128)(2,1)S(1)} async-done(((bf16[8,248,128]{2,1,0:T(8,128)(2,1)}), bf16[8,248,128]{2,1,0:T(8,128)(2,1)S(1)}, u32[]{:S(2)}, u32[]{:S(2)}) %all-to-all-start) | async-done | bytes 507936 | tf_op jit(solution)/shard_map/all_to_all | solution.py:183
  81.7 0.1 convert_reduce_fusion
  81.8 0.2 add_convert_fusion
  82.0 12.9 %all_to_all.15 = bf16[8,248,128]{2,1,0:T(8,128)(2,1)S(1)} all-to-all(bf16[8,248,128]{2,1,0:T(8,128)(2,1)S(1)} %add_convert_fusion), channel_id=1, replica_groups=mesh['x'=4,'core'=2,'u'=4,'v'=2,'hi'=2,'pair'=3,'duo'=2] {'core','x'}, dimensions={0} | all-to-all | bytes 1015808 | tf_op jit(solution)/shard_map/all_to_all | solution.py:188
  95.0 0.1 reduce_sum.22
  95.1 0.1 broadcast_in_dim.13
  95.1 20.4 %all_to_all.16.packed_ref = bf16[6,248,128]{2,1,0:T(8,128)(2,1)S(1)} all-to-all(bf16[6,248,128]{2,1,0:T(8,128)(2,1)S(1)} %broadcast_in_dim.13), channel_id=1, replica_groups=mesh['x'=4,'core'=2,'u'=4,'v'=2,'hi'=2,'pair'=3,'duo'=2] {'duo','pair'}, dimensions={0} | all-to-all | bytes 761856 | tf_op jit(solution)/shard_map/all_to_all | solution.py:18
  115.5 1.0 shard_map.49
  (7 shorter events, 0.1 us)
Async XLA Ops:
  0.0 1.6 %copy-start = (bf16[2,288,1728]{2,1,0:T(8,128)(2,1)S(1)}, bf16[2,288,1728]{2,1,0:T(8,128)(2,1)}, u32[]{:S(2)}) copy-start(bf16[2,288,1728]{2,1,0:T(8,128)(2,1)} %param.5) | copy-start | bytes 5971972
  3.4 6.6 %collective-permute-start.3 = (bf16[288,108]{1,0:T(8,128)(2,1)S(1)}, bf16[288,108]{1,0:T(8,128)(2,1)S(1)}, u32[]{:S(2)}, u32[]{:S(2)}) collective-permute-start(bf16[288,108]{1,0:T(8,128)(2,1)S(1)} %dynamic-slice_bitcast_fusion), channel_id=1, source_target_pairs={{0,1},{1,0},{2,3},{3,2},{4,5},{5,4},{6,7},{7,6},{8,9},{9,8},{10,11... | collective-permute-start | bytes 186632 | tf_op jit(solution)/shard_map/ppermute | solution.py:147
  10.1 23.3 %collective-permute-start.4 = (bf16[576,108]{1,0:T(8,128)(2,1)S(1)}, bf16[576,108]{1,0:T(8,128)(2,1)S(1)}, u32[]{:S(2)}, u32[]{:S(2)}) collective-permute-start(bf16[576,108]{1,0:T(8,128)(2,1)S(1)} %pad_maximum_fusion.3), channel_id=1, source_target_pairs={{0,6},{6,0},{1,7},{7,1},{2,8},{8,2},{3,9},{9,3},{4,10},{10,4},{5,1... | collective-permute-start | bytes 373256 | tf_op jit(solution)/shard_map/ppermute | solution.py:151
  26.4 13.2 %collective-permute-start = (bf16[2,384,128]{2,1,0:T(8,128)(2,1)S(1)}, bf16[2,384,128]{2,1,0:T(8,128)(2,1)S(1)}, u32[]{:S(2)}, u32[]{:S(2)}) collective-permute-start(bf16[2,384,128]{2,1,0:T(8,128)(2,1)S(1)} %get-tuple-element.8), channel_id=1, source_target_pairs={{0,1},{1,0},{2,3},{3,2},{4,5},{5,4},{6,7},{7,6},{8,9},{9,8},{10,11... | collective-permute-start | bytes 589832 | tf_op jit(solution)/shard_map/ppermute | solution.py:141
  29.9 18.5 %collective-permute-start.5 = (bf16[576,108]{1,0:T(8,128)(2,1)S(1)}, bf16[576,108]{1,0:T(8,128)(2,1)S(1)}, u32[]{:S(2)}, u32[]{:S(2)}) collective-permute-start(bf16[576,108]{1,0:T(8,128)(2,1)S(1)} %pad_maximum_fusion.3), channel_id=1, source_target_pairs={{0,12},{12,0},{1,13},{13,1},{2,14},{14,2},{3,15},{15,3},{4,16},{16... | collective-permute-start | bytes 373256 | tf_op jit(solution)/shard_map/ppermute | solution.py:158
  33.4 15.0 %collective-permute-start.6 = (bf16[576,108]{1,0:T(8,128)(2,1)S(1)}, bf16[576,108]{1,0:T(8,128)(2,1)S(1)}, u32[]{:S(2)}, u32[]{:S(2)}) collective-permute-start(bf16[576,108]{1,0:T(8,128)(2,1)S(1)} %collective-permute-done.4), channel_id=1, source_target_pairs={{0,12},{12,0},{1,13},{13,1},{2,14},{14,2},{3,15},{15,3},{4,16},{16... | collective-permute-start | bytes 373256 | tf_op jit(solution)/shard_map/ppermute | solution.py:158
  39.7 11.8 %collective-permute-start.1 = (bf16[2,384,128]{2,1,0:T(8,128)(2,1)S(1)}, bf16[2,384,128]{2,1,0:T(8,128)(2,1)S(1)}, u32[]{:S(2)}, u32[]{:S(2)}) collective-permute-start(bf16[2,384,128]{2,1,0:T(8,128)(2,1)S(1)} %get-tuple-element.15), channel_id=1, source_target_pairs={{0,2},{1,3},{2,4},{3,5},{4,6},{5,7},{6,8},{7,9},{8,10},{9,11},{10,... | collective-permute-start | bytes 589832 | tf_op jit(solution)/shard_map/ppermute | solution.py:156
  42.4 14.0 %collective-permute-start.2 = (bf16[2,384,128]{2,1,0:T(8,128)(2,1)S(1)}, bf16[2,384,128]{2,1,0:T(8,128)(2,1)S(1)}, u32[]{:S(2)}, u32[]{:S(2)}) collective-permute-start(bf16[2,384,128]{2,1,0:T(8,128)(2,1)S(1)} %get-tuple-element.13), channel_id=1, source_target_pairs={{2,0},{3,1},{4,2},{5,3},{6,4},{7,5},{8,6},{9,7},{10,8},{11,9},{0,1... | collective-permute-start | bytes 589832 | tf_op jit(solution)/shard_map/ppermute | solution.py:157
  48.9 17.6 %copy-start.1 = (bf16[2,8]{1,0:T(2,128)(2,1)S(1)}, bf16[2,8]{1,0:T(2,128)(2,1)}, u32[]{:S(2)}) copy-start(bf16[2,8]{1,0:T(2,128)(2,1)} %param.7) | copy-start | bytes 100
  59.0 22.8 %all-to-all-start = ((bf16[8,248,128]{2,1,0:T(8,128)(2,1)}), bf16[8,248,128]{2,1,0:T(8,128)(2,1)S(1)}, u32[]{:S(2)}, u32[]{:S(2)}) async-start(bf16[8,248,128]{2,1,0:T(8,128)(2,1)} %shard_map.48), calls=%async_computation | async-start | bytes 1015808 | tf_op jit(solution)/shard_map/all_to_all | solution.py:183
